TPU v7x, 128 devices: a whole 4x4x4 slice. The times are simulated.
128 devices in a mesh: dom: 16 (over y_lo, z, core), rep: 8 (over y_hi, x).
Axes of the slice: x: 4, y: 4 (y_hi: 2, y_lo: 2; y = y_hi * 2 + y_lo), z: 4, core: 2. Of those that a mesh axis runs over, the one named last changes fastest.
Arguments:
- node_features: bfloat16 [65536, 256], P(('dom', 'rep')), may hold values from -6 to 6
- weight: bfloat16 [256, 256], replicated, may hold values from -0.375 to 0.375
- cotangent: bfloat16 [65536, 256], P(('dom', 'rep')), may hold values from -6 to 6
- tile_row: int32 [16, 8, 512], P('dom', 'rep'), may hold values from 0 to 31
- tile_col: int32 [16, 8, 512], P('dom', 'rep'), may hold values from 0 to 63
- tile_values: bfloat16 [16, 8, 512, 128, 128], P('dom', 'rep'), may hold values from -0.0625 to 0.0625
- tile_count: int32 [16, 8], P('dom', 'rep'), may hold values from 128 to 512, as said below
Outputs:
- output: bfloat16 [65536, 256], P(('dom', 'rep'))
- grad_features: bfloat16 [65536, 256], P(('dom', 'rep'))
- grad_weight: float32 [256, 256], replicated
Inputs may be any that keep to these rules, and one draw needn't show every extreme that they name: Live slots are the first tile_count slots of each device's list; some device has all 512 slots live.
All inputs are finite; a program needn't handle non-finite values.
Results may differ from a plain program's by a relative error of at most 0.0061.
Values may be sent and summed in bfloat16 or wider, within the bound.
No kernel may reach another device: no remote copies, remote signals or barrier semaphores. Data moves between devices by JAX's collectives and lax.ppermute only.
A program may use at most 192 MiB of HBM per device.

v0:
```python
import jax
import jax.numpy as jnp
from jax import lax
from jax.sharding import PartitionSpec as P


def silu_slope(summed):
    sig = jax.nn.sigmoid(summed)
    return sig * (1.0 + summed * (1.0 - sig))


def tile_products(values, pick_index, place_index, active, source, out_blocks, flipped):
    slots = values.shape[0]
    feature_width = source.shape[2]
    per_turn = min(slots, 128)
    pattern = "tba,tbf->taf" if flipped else "tab,tbf->taf"

    def accumulate(turn_index, summed):
        first_slot = turn_index * per_turn
        block_values = lax.dynamic_slice_in_dim(values, first_slot, per_turn, 0)
        picks = lax.dynamic_slice_in_dim(pick_index, first_slot, per_turn, 0)
        picked = jnp.take(source, picks, axis=0)
        products = jnp.einsum(pattern, block_values, picked, preferred_element_type=jnp.float32)
        places = lax.dynamic_slice_in_dim(place_index, first_slot, per_turn, 0)
        enabled = lax.dynamic_slice_in_dim(active, first_slot, per_turn, 0)
        products = products * enabled.astype(jnp.float32)[:, None, None]
        return summed.at[places].add(products)

    initial = jnp.zeros((out_blocks, 128, feature_width), jnp.float32)
    summed = lax.fori_loop(0, slots // per_turn, accumulate, initial)
    return summed.reshape(out_blocks * 128, feature_width)


def body(node_features, weight, cotangent, tile_row, tile_col, tile_values, tile_count):
    rows_here = node_features.shape[0]
    feature_width = weight.shape[0]
    dom_size = lax.axis_size("dom")
    rep_size = lax.axis_size("rep")
    slots = tile_row.shape[2]
    row_index = tile_row.reshape(slots)
    col_index = tile_col.reshape(slots)
    values = tile_values.reshape(slots, 128, 128)
    active = lax.broadcasted_iota(jnp.int32, (slots,), 0) < tile_count.reshape(())
    projected = jnp.dot(node_features, weight, preferred_element_type=jnp.float32).astype(
        jnp.bfloat16
    )
    gathered = lax.all_gather(projected, "dom", axis=0, tiled=True)
    source = gathered.reshape(-1, 128, feature_width)
    part_blocks = rep_size * rows_here // 128
    partial_value = tile_products(values, col_index, row_index, active, source, part_blocks, False)
    summed = lax.psum_scatter(partial_value, "rep", scatter_dimension=0, tiled=True)
    output = jax.nn.silu(summed).astype(jnp.bfloat16)
    grad_own = (cotangent.astype(jnp.float32) * silu_slope(summed)).astype(jnp.bfloat16)
    grad_block = lax.all_gather(grad_own, "rep", axis=0, tiled=True)
    back_blocks = dom_size * rows_here // 128
    back_partial = tile_products(
        values,
        row_index,
        col_index,
        active,
        grad_block.reshape(-1, 128, feature_width),
        back_blocks,
        True,
    )
    grad_projected = lax.psum_scatter(back_partial, "dom", scatter_dimension=0, tiled=True).astype(
        jnp.bfloat16
    )
    grad_features = jnp.dot(grad_projected, weight.T, preferred_element_type=jnp.float32).astype(
        jnp.bfloat16
    )
    local_weight = jnp.dot(node_features.T, grad_projected, preferred_element_type=jnp.float32)
    grad_weight = lax.psum(local_weight, ("dom", "rep"))
    return (output, grad_features, grad_weight)


def solution(mesh):
    placed = (
        P(("dom", "rep"), None),
        P(),
        P(("dom", "rep"), None),
        P("dom", "rep", None),
        P("dom", "rep", None),
        P("dom", "rep", None, None, None),
        P("dom", "rep"),
    )
    return jax.shard_map(
        body,
        mesh=mesh,
        in_specs=placed,
        out_specs=(P(("dom", "rep"), None), P(("dom", "rep"), None), P()),
        check_vma=False,
    )
```

profile of v0, /device:TPU:1, one launch (start us, length us, event | category | flops | bytes accessed | tf_op | source)
XLA Modules:
  0.0 908.4 jit_solution(10777865380881318707)
XLA Ops:
  10.7 40.7 %all-gather.3.cloned.1.call-done = bf16[8192,256]{1,0:T(8,128)(2,1)} async-done(((bf16[512,256]{1,0:T(8,128)(2,1)}), bf16[8192,256]{1,0:T(8,128)(2,1)}) %all-gather.3.cloned.1.call-update) | async-done | bytes 4194320 | tf_op jit(solution)/shard_map/all_gather | solution.py:47
  53.8 244.0 %while.26 = (s32[]{:T(128)}, f32[32,128,256]{2,1,0:T(8,128)}, s32[512]{0:T(512)}, bf16[512,128,128]{2,1,0:T(8,128)(2,1)}, s32[512]{0:T(512)}, /*index=5*/bf16[64...) while((s32[]{:T(128)}, f32[32,128,256]{2,1,0:T(8,128)}, ...), condition=%wide.region_2.3_spmd, body=%wide.region_0.2_spmd.sunk | while | flops 1086327040 | bytes 96478248 | solution.py:30
  54.6 8.8 gather_fusion
  63.4 12.8 %convolution_multiply_fusion.4 = f32[128,128,256]{2,1,0:T(8,128)} fusion(f32[128]{0:T(128)S(1)} %get-tuple-element.384, bf16[128,128,256]{2,1,0:T(8,128)(2,1)} %gather_fusion, pred[128]{0:T(512)(128)(4,1)S(1)} %get-tuple-element.386, bf16[512,128,128]{2,1,0:T(8,128)(2,1)} %get-tuple-element.422, s32[]{:T(128)S(6)} %select_n.85), kind=kOutput, calls=%fused_computation.4.clone.1 | convolution fusion | flops 1082130432 | bytes 29360772 | tf_op jit(solution)/shard_map/while/body/eval_jaxpr/tab,tbf->taf/dot_general | solution.py:23
  76.9 37.9 %scatter_fusion = f32[32,128,256]{2,1,0:T(8,128)} fusion(f32[32,128,256]{2,1,0:T(8,128)} %get-tuple-element.409, s32[128]{0:T(128)S(1)} %compare_select_fusion.8, f32[128,128,256]{2,1,0:T(8,128)} %convolution_multiply_fusion.4), kind=kCustom, calls=%fused_computation.2.clone.1 | custom fusion | flops 4194304 | bytes 50332160 | tf_op jit(solution)/shard_map/while/body/eval_jaxpr/scatter-add | solution.py:27
  115.6 8.8 gather_fusion
  124.3 12.8 %convolution_multiply_fusion.4 = f32[128,128,256]{2,1,0:T(8,128)} fusion(f32[128]{0:T(128)S(1)} %get-tuple-element.384, bf16[128,128,256]{2,1,0:T(8,128)(2,1)} %gather_fusion, pred[128]{0:T(512)(128)(4,1)S(1)} %get-tuple-element.386, bf16[512,128,128]{2,1,0:T(8,128)(2,1)} %get-tuple-element.422, s32[]{:T(128)S(6)} %select_n.85), kind=kOutput, calls=%fused_computation.4.clone.1 | convolution fusion | flops 1082130432 | bytes 29360772 | tf_op jit(solution)/shard_map/while/body/eval_jaxpr/tab,tbf->taf/dot_general | solution.py:23
  137.9 37.9 %scatter_fusion = f32[32,128,256]{2,1,0:T(8,128)} fusion(f32[32,128,256]{2,1,0:T(8,128)} %get-tuple-element.409, s32[128]{0:T(128)S(1)} %compare_select_fusion.8, f32[128,128,256]{2,1,0:T(8,128)} %convolution_multiply_fusion.4), kind=kCustom, calls=%fused_computation.2.clone.1 | custom fusion | flops 4194304 | bytes 50332160 | tf_op jit(solution)/shard_map/while/body/eval_jaxpr/scatter-add | solution.py:27
  176.6 8.8 gather_fusion
  185.3 12.8 %convolution_multiply_fusion.4 = f32[128,128,256]{2,1,0:T(8,128)} fusion(f32[128]{0:T(128)S(1)} %get-tuple-element.384, bf16[128,128,256]{2,1,0:T(8,128)(2,1)} %gather_fusion, pred[128]{0:T(512)(128)(4,1)S(1)} %get-tuple-element.386, bf16[512,128,128]{2,1,0:T(8,128)(2,1)} %get-tuple-element.422, s32[]{:T(128)S(6)} %select_n.85), kind=kOutput, calls=%fused_computation.4.clone.1 | convolution fusion | flops 1082130432 | bytes 29360772 | tf_op jit(solution)/shard_map/while/body/eval_jaxpr/tab,tbf->taf/dot_general | solution.py:23
  198.9 37.9 %scatter_fusion = f32[32,128,256]{2,1,0:T(8,128)} fusion(f32[32,128,256]{2,1,0:T(8,128)} %get-tuple-element.409, s32[128]{0:T(128)S(1)} %compare_select_fusion.8, f32[128,128,256]{2,1,0:T(8,128)} %convolution_multiply_fusion.4), kind=kCustom, calls=%fused_computation.2.clone.1 | custom fusion | flops 4194304 | bytes 50332160 | tf_op jit(solution)/shard_map/while/body/eval_jaxpr/scatter-add | solution.py:27
  237.6 8.8 gather_fusion
  246.3 12.8 %convolution_multiply_fusion.4 = f32[128,128,256]{2,1,0:T(8,128)} fusion(f32[128]{0:T(128)S(1)} %get-tuple-element.384, bf16[128,128,256]{2,1,0:T(8,128)(2,1)} %gather_fusion, pred[128]{0:T(512)(128)(4,1)S(1)} %get-tuple-element.386, bf16[512,128,128]{2,1,0:T(8,128)(2,1)} %get-tuple-element.422, s32[]{:T(128)S(6)} %select_n.85), kind=kOutput, calls=%fused_computation.4.clone.1 | convolution fusion | flops 1082130432 | bytes 29360772 | tf_op jit(solution)/shard_map/while/body/eval_jaxpr/tab,tbf->taf/dot_general | solution.py:23
  259.9 37.9 %scatter_fusion = f32[32,128,256]{2,1,0:T(8,128)} fusion(f32[32,128,256]{2,1,0:T(8,128)} %get-tuple-element.409, s32[128]{0:T(128)S(1)} %compare_select_fusion.8, f32[128,128,256]{2,1,0:T(8,128)} %convolution_multiply_fusion.4), kind=kCustom, calls=%fused_computation.2.clone.1 | custom fusion | flops 4194304 | bytes 50332160 | tf_op jit(solution)/shard_map/while/body/eval_jaxpr/scatter-add | solution.py:27
  297.9 83.9 %reduce-scatter.3.cloned.1.call-done = f32[512,256]{1,0:T(8,128)} async-done(((f32[4096,256]{1,0:T(8,128)}), f32[512,256]{1,0:T(8,128)}) %reduce-scatter.3.cloned.1.call-update) | async-done | bytes 524304 | tf_op jit(solution)/shard_map/reduce_scatter | solution.py:51
  384.1 22.4 %copy.10 = bf16[1,1,512,128,128]{3,4,2,1,0:T(8,128)(2,1)} copy(bf16[1,1,512,128,128]{4,3,2,1,0:T(8,128)(2,1)} %bitcast.21) | data formatting | bytes 33554432 | tf_op args[5]
  406.5 31.9 %all-gather.5.cloned.1.call-done = bf16[4096,256]{1,0:T(8,128)(2,1)} async-done(((bf16[512,256]{1,0:T(8,128)(2,1)}), bf16[4096,256]{1,0:T(8,128)(2,1)}) %all-gather.5.cloned.1.call-update) | async-done | bytes 2097168 | tf_op jit(solution)/shard_map/all_gather | solution.py:54
  442.6 237.0 %while.27 = (s32[]{:T(128)}, f32[64,128,256]{2,1,0:T(8,128)}, s32[512]{0:T(512)}, bf16[512,128,128]{1,2,0:T(8,128)(2,1)}, s32[512]{0:T(512)}, /*index=5*/bf16[32...) while((s32[]{:T(128)}, f32[64,128,256]{2,1,0:T(8,128)}, ...), condition=%wide.region_6.7_spmd, body=%wide.region_4.6_spmd.sunk | while | flops 1086327040 | bytes 96478248 | solution.py:30
  443.4 6.6 gather_fusion.1
  450.0 12.8 %convolution_multiply_fusion.5 = f32[128,128,256]{2,1,0:T(8,128)} fusion(f32[128]{0:T(128)S(1)} %get-tuple-element.394, bf16[128,128,256]{2,1,0:T(8,128)(2,1)} %gather_fusion.1, pred[128]{0:T(512)(128)(4,1)S(1)} %get-tuple-element.396, bf16[512,128,128]{1,2,0:T(8,128)(2,1)} %get-tuple-element.455, s32[]{:T(128)S(6)} %select_n.88), kind=kOutput, calls=%fused_computation.16.clone.1 | convolution fusion | flops 1082130432 | bytes 29360772 | tf_op jit(solution)/shard_map/while/body/eval_jaxpr/tba,tbf->taf/dot_general | solution.py:23
  463.5 38.2 %scatter_fusion.1 = f32[64,128,256]{2,1,0:T(8,128)} fusion(f32[64,128,256]{2,1,0:T(8,128)} %get-tuple-element.442, s32[128]{0:T(128)S(1)} %compare_select_fusion.9, f32[128,128,256]{2,1,0:T(8,128)} %convolution_multiply_fusion.5), kind=kCustom, calls=%fused_computation.3.clone.1 | custom fusion | flops 4194304 | bytes 50332160 | tf_op jit(solution)/shard_map/while/body/eval_jaxpr/scatter-add | solution.py:27
  502.5 6.6 gather_fusion.1
  509.1 12.8 %convolution_multiply_fusion.5 = f32[128,128,256]{2,1,0:T(8,128)} fusion(f32[128]{0:T(128)S(1)} %get-tuple-element.394, bf16[128,128,256]{2,1,0:T(8,128)(2,1)} %gather_fusion.1, pred[128]{0:T(512)(128)(4,1)S(1)} %get-tuple-element.396, bf16[512,128,128]{1,2,0:T(8,128)(2,1)} %get-tuple-element.455, s32[]{:T(128)S(6)} %select_n.88), kind=kOutput, calls=%fused_computation.16.clone.1 | convolution fusion | flops 1082130432 | bytes 29360772 | tf_op jit(solution)/shard_map/while/body/eval_jaxpr/tba,tbf->taf/dot_general | solution.py:23
  522.6 38.4 %scatter_fusion.1 = f32[64,128,256]{2,1,0:T(8,128)} fusion(f32[64,128,256]{2,1,0:T(8,128)} %get-tuple-element.442, s32[128]{0:T(128)S(1)} %compare_select_fusion.9, f32[128,128,256]{2,1,0:T(8,128)} %convolution_multiply_fusion.5), kind=kCustom, calls=%fused_computation.3.clone.1 | custom fusion | flops 4194304 | bytes 50332160 | tf_op jit(solution)/shard_map/while/body/eval_jaxpr/scatter-add | solution.py:27
  561.8 6.6 gather_fusion.1
  568.3 12.8 %convolution_multiply_fusion.5 = f32[128,128,256]{2,1,0:T(8,128)} fusion(f32[128]{0:T(128)S(1)} %get-tuple-element.394, bf16[128,128,256]{2,1,0:T(8,128)(2,1)} %gather_fusion.1, pred[128]{0:T(512)(128)(4,1)S(1)} %get-tuple-element.396, bf16[512,128,128]{1,2,0:T(8,128)(2,1)} %get-tuple-element.455, s32[]{:T(128)S(6)} %select_n.88), kind=kOutput, calls=%fused_computation.16.clone.1 | convolution fusion | flops 1082130432 | bytes 29360772 | tf_op jit(solution)/shard_map/while/body/eval_jaxpr/tba,tbf->taf/dot_general | solution.py:23
  581.9 38.4 %scatter_fusion.1 = f32[64,128,256]{2,1,0:T(8,128)} fusion(f32[64,128,256]{2,1,0:T(8,128)} %get-tuple-element.442, s32[128]{0:T(128)S(1)} %compare_select_fusion.9, f32[128,128,256]{2,1,0:T(8,128)} %convolution_multiply_fusion.5), kind=kCustom, calls=%fused_computation.3.clone.1 | custom fusion | flops 4194304 | bytes 50332160 | tf_op jit(solution)/shard_map/while/body/eval_jaxpr/scatter-add | solution.py:27
  621.0 6.6 gather_fusion.1
  627.6 12.8 %convolution_multiply_fusion.5 = f32[128,128,256]{2,1,0:T(8,128)} fusion(f32[128]{0:T(128)S(1)} %get-tuple-element.394, bf16[128,128,256]{2,1,0:T(8,128)(2,1)} %gather_fusion.1, pred[128]{0:T(512)(128)(4,1)S(1)} %get-tuple-element.396, bf16[512,128,128]{1,2,0:T(8,128)(2,1)} %get-tuple-element.455, s32[]{:T(128)S(6)} %select_n.88), kind=kOutput, calls=%fused_computation.16.clone.1 | convolution fusion | flops 1082130432 | bytes 29360772 | tf_op jit(solution)/shard_map/while/body/eval_jaxpr/tba,tbf->taf/dot_general | solution.py:23
  641.2 38.5 %scatter_fusion.1 = f32[64,128,256]{2,1,0:T(8,128)} fusion(f32[64,128,256]{2,1,0:T(8,128)} %get-tuple-element.442, s32[128]{0:T(128)S(1)} %compare_select_fusion.9, f32[128,128,256]{2,1,0:T(8,128)} %convolution_multiply_fusion.5), kind=kCustom, calls=%fused_computation.3.clone.1 | custom fusion | flops 4194304 | bytes 50332160 | tf_op jit(solution)/shard_map/while/body/eval_jaxpr/scatter-add | solution.py:27
  679.7 71.6 %reduce-scatter.5.cloned.1.call-done = f32[512,256]{1,0:T(8,128)} async-done(((f32[8192,256]{1,0:T(8,128)}), f32[512,256]{1,0:T(8,128)}) %reduce-scatter.5.cloned.1.call-update) | async-done | bytes 524304 | tf_op jit(solution)/shard_map/reduce_scatter | solution.py:65
  755.4 144.8 %all-reduce.2.cloned.1.call-done = f32[256,256]{0,1:T(8,128)} async-done(((f32[256,256]{0,1:T(8,128)}), f32[256,256]{0,1:T(8,128)}) %all-reduce.2.cloned.1.call-update) | async-done | bytes 262160 | tf_op jit(solution)/shard_map/psum | solution.py:72
  (50 shorter events, 29.9 us)
Async XLA Ops:
  7.2 1.0 copy-start
  7.2 44.2 %all-gather.3.cloned.1.call-start = ((), (), s32[]{:S(2)}) async-start(), calls=%async_computation.2 | async-start | bytes 4456448 | tf_op jit(solution)/shard_map/all_gather | solution.py:47
  10.0 371.8 %reduce-scatter.3.cloned.1.call-start = ((), (), s32[]{:S(2)}) async-start(), calls=%async_computation.3 | async-start | bytes 4718592 | tf_op jit(solution)/shard_map/reduce_scatter | solution.py:51
  53.8 328.0 %copy-start.3 = (bf16[512,256]{1,0:T(8,128)(2,1)S(1)}, bf16[512,256]{1,0:T(8,128)(2,1)}, u32[]{:S(2)}) copy-start(bf16[512,256]{1,0:T(8,128)(2,1)} %param.13) | copy-start | bytes 786436
  297.8 140.6 %all-gather.5.cloned.1.call-start = ((), (), s32[]{:S(2)}) async-start(), calls=%async_computation.4 | async-start | bytes 2359296 | tf_op jit(solution)/shard_map/all_gather | solution.py:54
  383.9 367.4 %reduce-scatter.5.cloned.1.call-start = ((), (), s32[]{:S(2)}) async-start(), calls=%async_computation.5 | async-start | bytes 8912896 | tf_op jit(solution)/shard_map/reduce_scatter | solution.py:65
  438.4 4.2 copy-start.1
  679.7 73.7 %copy-start.2 = (bf16[256,256]{1,0:T(8,128)(2,1)S(1)}, bf16[256,256]{1,0:T(8,128)(2,1)}, u32[]{:S(2)}) copy-start(bf16[256,256]{1,0:T(8,128)(2,1)} %param.12) | copy-start | bytes 393220
  679.7 220.4 %all-reduce.2.cloned.1.call-start = ((), (), s32[]{:S(2)}) async-start(), calls=%async_computation.6 | async-start | bytes 524288 | tf_op jit(solution)/shard_map/psum | solution.py:72
Sparse Core Ops, SparseCore 0:
  10.3 41.0 all-gather.2
  298.0 83.7 reduce-scatter.2
  384.7 53.6 all-gather.4
  679.8 71.4 reduce-scatter.4
  756.5 143.6 all-reduce.1
where the time goes:
time: 911 us; the launch traced here: 908 us
  waiting for transfers between devices  373 us (41%)
  other arithmetic  319 us (35%)
  matrix products  108 us (12%)
  local copies, waits for them, and re-layouts  93 us (10%)
  between operations  14.5 us (2%)
    scatter-add x8, other arithmetic, accumulate(): return summed.at[places].add(products)  305 us
    psum x1, waiting for transfers between devices, body(): grad_weight = lax.psum(local_weight, ('dom', 'rep'))  145 us
    dot_general x8, matrix products, accumulate(): jnp.einsum(pattern, block_values, picked, preferred_element_type=jnp.floa...  103 us
    reduce_scatter x1, waiting for transfers between devices, body(): lax.psum_scatter(partial_value, 'rep', scatter_dimension=0, tiled=True)  83.9 us
    reduce_scatter x1, waiting for transfers between devices, body(): lax.psum_scatter(back_partial, 'dom', scatter_dimension=0, tiled=True)  71.6 us
    gather x8, local copies, waits for them, and re-layouts, accumulate(): picked = jnp.take(source, picks, axis=0)  61.3 us
    all_gather x1, waiting for transfers between devices, body(): gathered = lax.all_gather(projected, 'dom', axis=0, tiled=True)  40.7 us
    all_gather x1, waiting for transfers between devices, body(): grad_block = lax.all_gather(grad_own, 'rep', axis=0, tiled=True)  31.9 us
  transfers between devices with their start and end apart: 5, of which 5 were waited for; matrix products, arithmetic and copies ran while one was open for 3% of the time, Pallas kernels for 0%

commit v1 on v0

v1 whole, which is shorter than its diff:
```python
import functools

import jax
import jax.numpy as jnp
from jax import lax
from jax.experimental import pallas as pl
from jax.experimental.pallas import tpu as pltpu
from jax.sharding import PartitionSpec as P

BLOCK = 128
UNROLL = 16


def pair_plan(place, pick, count, places, pairs_max):
    slots = place.shape[0]
    slot = jnp.arange(slots, dtype=jnp.int32)
    live = slot < count
    key = jnp.where(live, place, places)
    earlier = (key[:, None] == key[None, :]) & (slot[None, :] < slot[:, None])
    rank = jnp.sum(earlier, axis=1, dtype=jnp.int32)
    block = jnp.arange(places, dtype=jnp.int32)
    per_block = jnp.sum(key[None, :] == block[:, None], axis=1, dtype=jnp.int32)
    pairs = (per_block + 1) // 2
    before = jnp.sum(jnp.where(block[None, :] < block[:, None], pairs[None, :], 0), axis=1, dtype=jnp.int32)
    first = jnp.sum(jnp.where(key[:, None] == block[None, :], before[None, :], 0), axis=1, dtype=jnp.int32)
    position = jnp.where(live, 2 * first + rank, -1)
    half = jnp.arange(2 * pairs_max, dtype=jnp.int32)
    hit = half[:, None] == position[None, :]
    tile = jnp.sum(jnp.where(hit, slot[None, :] - slots, 0), axis=1, dtype=jnp.int32) + slots
    picked = jnp.sum(jnp.where(hit, pick[None, :], 0), axis=1, dtype=jnp.int32)
    placed = jnp.sum(jnp.where(hit, place[None, :], 0), axis=1, dtype=jnp.int32)
    return jnp.sum(pairs).reshape(1), tile, picked, placed


def load_kernel(tiles_ref, held_ref, sems):
    slots = tiles_ref.shape[0]
    pieces = sems.shape[0]
    piece = slots // pieces

    def copy(i):
        window = pl.ds(i * piece, piece)
        return pltpu.make_async_copy(tiles_ref.at[window], held_ref.at[window], sems.at[i])

    for i in range(pieces):
        copy(i).start()
    held_ref[slots] = jnp.zeros(held_ref.shape[1:], held_ref.dtype)
    for i in range(pieces):
        copy(i).wait()


def load_tiles(tiles):
    slots = tiles.shape[0]
    return pl.pallas_call(
        load_kernel,
        out_shape=pltpu.VMEM((slots + 1, BLOCK, BLOCK), tiles.dtype),
        in_specs=[pl.BlockSpec(memory_space=pl.ANY)],
        out_specs=pl.BlockSpec(memory_space=pltpu.VMEM),
        scratch_shapes=[pltpu.SemaphoreType.DMA((8,))],
        compiler_params=pltpu.CompilerParams(vmem_limit_bytes=1 << 20),
        cost_estimate=pl.CostEstimate(flops=0, bytes_accessed=2 * tiles.size, transcendentals=0),
        name="load_tiles",
    )(tiles)


def spread_kernel(flipped, pairs_ref, tile_ref, pick_ref, place_ref, tiles_ref, source_ref, *refs):
    *out_refs, total_ref = refs
    total_ref[...] = jnp.zeros_like(total_ref)

    def rows_of(index):
        return source_ref[pl.ds(pl.multiple_of(index * 64, 64), BLOCK), :]

    @pl.loop(0, (pairs_ref[0] + UNROLL - 1) // UNROLL)
    def _(turn):
        for step in range(UNROLL):
            first = (turn * UNROLL + step) * 2
            rows = jnp.concatenate([rows_of(pick_ref[first]), rows_of(pick_ref[first + 1])], axis=0)
            tiles = [tiles_ref[tile_ref[first]], tiles_ref[tile_ref[first + 1]]]
            if flipped:
                product = lax.dot_general(
                    jnp.concatenate(tiles, axis=0), rows, (((0,), (0,)), ((), ())), preferred_element_type=jnp.float32
                )
            else:
                product = jnp.dot(jnp.concatenate(tiles, axis=1), rows, preferred_element_type=jnp.float32)
            total_ref[place_ref[first]] += product

    part = total_ref.shape[0] // len(out_refs)
    for i, out_ref in enumerate(out_refs):
        out_ref[...] = total_ref[i * part : (i + 1) * part].astype(out_ref.dtype)


def spread(plan, tiles, source, places, parts, flipped):
    width = source.shape[1]
    return pl.pallas_call(
        functools.partial(spread_kernel, flipped),
        out_shape=[jax.ShapeDtypeStruct((places // parts, BLOCK, width), jnp.bfloat16)] * parts,
        in_specs=[pl.BlockSpec(memory_space=pltpu.SMEM)] * 4 + [pl.BlockSpec(memory_space=pltpu.VMEM)] * 2,
        out_specs=[pl.BlockSpec(memory_space=pltpu.VMEM)] * parts,
        scratch_shapes=[pltpu.VMEM((places, BLOCK, width), jnp.float32)],
        compiler_params=pltpu.CompilerParams(vmem_limit_bytes=24 << 20),
        cost_estimate=pl.CostEstimate(
            flops=2 * tiles.size * width, bytes_accessed=2 * (tiles.size + source.size), transcendentals=0
        ),
        name="spread_back" if flipped else "spread_forward",
    )(*plan, tiles, source)


def split(value):
    high = value.astype(jnp.bfloat16)
    return high, (value - high.astype(jnp.float32)).astype(jnp.bfloat16)


def middle_kernel(parts_ref, weight_ref, cotangent_ref, out_ref, send_ref):
    members, rows, width = parts_ref.shape
    share = width // members
    mixed = parts_ref[0].astype(jnp.float32)
    for member in range(1, members):
        mixed += parts_ref[member].astype(jnp.float32)
    high, low = split(mixed)
    weight = weight_ref[...]
    summed = jnp.dot(high, weight, preferred_element_type=jnp.float32)
    summed += jnp.dot(low, weight, preferred_element_type=jnp.float32)
    sig = jax.nn.sigmoid(summed)
    out_ref[...] = (summed * sig).astype(out_ref.dtype)
    slope = sig * (1.0 + summed * (1.0 - sig))
    grad = (cotangent_ref[...].astype(jnp.float32) * slope).astype(jnp.bfloat16)
    across = (((0,), (0,)), ((), ()))
    term = lax.dot_general(high, grad, across, preferred_element_type=jnp.float32)
    term += lax.dot_general(low, grad, across, preferred_element_type=jnp.float32)
    term_high, term_low = split(term)
    for member in range(members):
        mine = slice(member * share, (member + 1) * share)
        send_ref[member, :rows, :] = grad
        send_ref[member, rows : rows + share, :] = term_high[mine]
        send_ref[member, rows + share :, :] = term_low[mine]


def join_kernel(own_ref, other_ref, term_ref, send_ref):
    rows = own_ref.shape[1]
    share = term_ref.shape[0]
    send_ref[0, :rows, :] = (own_ref[0].astype(jnp.float32) + other_ref[0].astype(jnp.float32)).astype(jnp.bfloat16)
    high, low = split(term_ref[...])
    send_ref[0, rows : rows + share, :] = high
    send_ref[0, rows + share :, :] = low


def last_kernel(parts_ref, weight_ref, out_ref, term_ref):
    members = parts_ref.shape[0]
    rows = out_ref.shape[0]
    share = term_ref.shape[1]
    total = parts_ref[0].astype(jnp.float32)
    for member in range(1, members):
        total += parts_ref[member].astype(jnp.float32)
    grad = total[:rows].astype(jnp.bfloat16)
    out_ref[...] = lax.dot_general(
        grad, weight_ref[...], (((1,), (1,)), ((), ())), preferred_element_type=jnp.float32
    ).astype(out_ref.dtype)
    term = total[rows : rows + share] + total[rows + share :]
    for member in range(term_ref.shape[0]):
        term_ref[member] = term


def body(node_features, weight, cotangent, tile_row, tile_col, tile_values, tile_count):
    rows, width = node_features.shape
    dom_size = lax.axis_size("dom")
    rep_size = lax.axis_size("rep")
    slots = tile_row.shape[2]
    own = rows // BLOCK
    share = width // rep_size
    wide = rows + 2 * share
    params = pltpu.CompilerParams(vmem_limit_bytes=24 << 20)
    row_index = tile_row.reshape(slots)
    col_index = tile_col.reshape(slots)
    count = tile_count.reshape(())
    tiles = load_tiles(tile_values.reshape(slots, BLOCK, BLOCK))
    parity = lax.axis_index("dom") % 2

    gathered = lax.all_gather(node_features, "dom", axis=0, tiled=True)

    row_blocks = rep_size * own
    col_blocks = dom_size * own

    def padded(places):
        return -(-((slots + places) // 2) // UNROLL) * UNROLL

    forward_plan = pair_plan(row_index, col_index * (BLOCK // 64), count, row_blocks, padded(row_blocks))
    owner = col_index // own
    col_place = ((owner + parity) % 2) * (col_blocks // 2) + (owner // 2) * own + col_index % own
    row_pick = (row_index // own) * (wide // 64) + (row_index % own) * (BLOCK // 64)
    back_plan = pair_plan(col_place, row_pick, count, col_blocks, padded(col_blocks))

    (partial,) = spread(forward_plan, tiles, gathered, row_blocks, 1, False)
    parts = lax.all_to_all(partial.reshape(rep_size, rows, width), "rep", 0, 0, tiled=True)
    output, grads_out = pl.pallas_call(
        middle_kernel,
        out_shape=(
            jax.ShapeDtypeStruct((rows, width), jnp.bfloat16),
            jax.ShapeDtypeStruct((rep_size, wide, width), jnp.bfloat16),
        ),
        compiler_params=params,
        name="middle",
    )(parts, weight, cotangent)
    grads = lax.all_to_all(grads_out, "rep", 0, 0, tiled=True)

    term = jnp.sum(grads[:, rows:].astype(jnp.float32), axis=0)
    term = term[:share] + term[share:]
    swap = [(place, place ^ 1) for place in range(dom_size)]
    term = term + lax.ppermute(term, "dom", swap)

    back = spread(back_plan, tiles, grads.reshape(rep_size * wide, width), col_blocks, 2, True)
    mine, other = (half.reshape(dom_size // 2, rows, width) for half in back)
    other = lax.ppermute(other, "dom", swap)
    joined = pl.pallas_call(
        join_kernel,
        grid=(dom_size // 2,),
        out_shape=jax.ShapeDtypeStruct((dom_size // 2, wide, width), jnp.bfloat16),
        in_specs=[
            pl.BlockSpec((1, rows, width), lambda i: (i, 0, 0)),
            pl.BlockSpec((1, rows, width), lambda i: (i, 0, 0)),
            pl.BlockSpec((share, width), lambda i: (0, 0)),
        ],
        out_specs=pl.BlockSpec((1, wide, width), lambda i: (i, 0, 0)),
        compiler_params=params,
        name="join",
    )(mine, other, term)
    same_core = [list(range(core, dom_size, 2)) for core in range(2)]
    back_parts = lax.all_to_all(joined, "dom", 0, 0, axis_index_groups=same_core, tiled=True)
    grad_features, term_out = pl.pallas_call(
        last_kernel,
        out_shape=(
            jax.ShapeDtypeStruct((rows, width), jnp.bfloat16),
            jax.ShapeDtypeStruct((rep_size, share, width), jnp.float32),
        ),
        compiler_params=params,
        name="last",
    )(back_parts, weight)
    grad_weight = lax.all_to_all(term_out, "rep", 0, 0, tiled=True).reshape(width, width)
    return (output, grad_features, grad_weight)


def solution(mesh):
    placed = (
        P(("dom", "rep"), None),
        P(),
        P(("dom", "rep"), None),
        P("dom", "rep", None),
        P("dom", "rep", None),
        P("dom", "rep", None, None, None),
        P("dom", "rep"),
    )
    return jax.shard_map(
        body,
        mesh=mesh,
        in_specs=placed,
        out_specs=(P(("dom", "rep"), None), P(("dom", "rep"), None), P()),
        check_vma=False,
    )
```

time: 911 us -> 222 us (0.24)
  other arithmetic: 319 us -> 3.65 us
  waiting for transfers between devices: 373 us -> 61.7 us
  matrix products: 108 us -> 0 us
  blocking collectives: 0 us -> 87.7 us
  local copies, waits for them, and re-layouts: 93 us -> 27.4 us
  Pallas kernels: 0 us -> 14.3 us
  starting transfers between devices: 0.39 us -> 9.97 us
    scatter-add x8 -> x0, other arithmetic: 305 us -> none  [accumulate(): return summed.at[places].add(products)]
    reduce_scatter x2 -> x0, waiting for transfers between devices: 155 us -> none  [the longest x1 83.9 us: body(): lax.psum_scatter(partial_value, 'rep', scatter_dimension=0, tiled=True)]
    psum x1 -> x0, waiting for transfers between devices: 145 us -> none  [body(): grad_weight = lax.psum(local_weight, ('dom', 'rep'))]
    dot_general x11 -> x0, matrix products: 108 us -> none  [the longest x8 103 us: accumulate(): jnp.einsum(pattern, block_values, picked, preferred_element_type=jnp.floa...]
    all_to_all x0 -> x3, blocking collectives: none -> 87.7 us  [the longest x1 39.3 us: body(): lax.all_to_all(partial.reshape(rep_size, rows, width), 'rep', 0, 0, tiled...]
    gather x8 -> x0, local copies, waits for them, and re-layouts: 61.3 us -> none  [accumulate(): picked = jnp.take(source, picks, axis=0)]
    all_gather x2 -> x1, waiting for transfers between devices: 72.6 us -> 26.5 us  [body(): gathered = lax.all_gather(node_features, 'dom', axis=0, tiled=True)]
    all_to_all x0 -> x1, waiting for transfers between devices: none -> 30.8 us  [body(): grads = lax.all_to_all(grads_out, 'rep', 0, 0, tiled=True)]
  transfers between devices with their start and end apart: 5 -> 4, of which waited for: 5 -> 3; matrix products, arithmetic and copies ran while one was open for 3% -> 2% of each run, Pallas kernels for 0% -> 1%
where the time goes in v1:
time: 222 us; the launch traced here: 220 us
  blocking collectives  87.7 us (40%)
  waiting for transfers between devices  61.7 us (28%)
  local copies, waits for them, and re-layouts  27.4 us (12%)
  between operations  14.8 us (7%)
  Pallas kernels  14.3 us (6%)
  starting transfers between devices  9.97 us (4%)
  other arithmetic  3.65 us (2%)
    all_to_all x1, blocking collectives, body(): lax.all_to_all(partial.reshape(rep_size, rows, width), 'rep', 0, 0, tiled...  39.3 us
    all_to_all x1, blocking collectives, body(): lax.all_to_all(joined, 'dom', 0, 0, axis_index_groups=same_core, tiled=True)  31.5 us
    all_to_all x1, waiting for transfers between devices, body(): grads = lax.all_to_all(grads_out, 'rep', 0, 0, tiled=True)  30.8 us
    unnamed x21, local copies, waits for them, and re-layouts  27.4 us
    all_gather x1, waiting for transfers between devices, body(): gathered = lax.all_gather(node_features, 'dom', axis=0, tiled=True)  26.5 us
    all_to_all x1, blocking collectives, body(): lax.all_to_all(term_out, 'rep', 0, 0, tiled=True).reshape(width, width)  17 us
    pallas_call x2, Pallas kernels, spread(): pl.pallas_call(functools.partial(spread_kernel, flipped), out_shape=[jax....  9.97 us
    ppermute x1, starting transfers between devices, body(): other = lax.ppermute(other, 'dom', swap)  6.21 us
  transfers between devices with their start and end apart: 4, of which 3 were waited for; matrix products, arithmetic and copies ran while one was open for 2% of the time, Pallas kernels for 1%

profile of v1, /device:TPU:1, one launch (start us, length us, event | category | flops | bytes accessed | tf_op | source)
XLA Modules:
  0.0 219.5 jit_solution(7058596195059957004)
XLA Ops:
  7.2 0.7 all-gather.2.cloned.1.call-update
  8.6 5.8 %copy-done.3 = bf16[1,1,512,128,128]{4,3,2,1,0:T(8,128)(2,1)S(1)} copy-done((bf16[1,1,512,128,128]{4,3,2,1,0:T(8,128)(2,1)S(1)}, bf16[1,1,512,128,128]{4,3,2,1,0:T(8,128)(2,1)}, u32[]{:S(2)}) %copy-start.3) | copy-done | bytes 16777240
  14.3 1.2 load_tiles.1.tiles_ref
  15.6 5.7 %copy-done = bf16[513,128,128]{2,1,0:T(8,128)(2,1)} copy-done((bf16[513,128,128]{2,1,0:T(8,128)(2,1)}, bf16[513,128,128]{2,1,0:T(8,128)(2,1)S(1)}, u32[]{:S(2)}) %copy-start) | copy-done | bytes 16810008
  21.3 0.1 convert_reduce_fusion.3
  21.4 0.6 fusion.17
  22.1 0.1 select_reduce_fusion.8
  22.3 0.3 convert_reduce_fusion
  22.6 0.1 convert_reduce_fusion.4
  22.7 0.6 fusion.19
  23.3 0.1 select_reduce_fusion.9
  23.5 0.3 convert_reduce_fusion.1
  23.8 0.5 select_reduce_fusion.3
  24.3 26.5 %all-gather.2.cloned.1.call-done.source_ref = bf16[8192,256]{1,0:T(8,128)(2,1)} async-done(((bf16[512,256]{1,0:T(8,128)(2,1)}), bf16[8192,256]{1,0:T(8,128)(2,1)}) %all-gather.2.cloned.1.call-update) | async-done | bytes 4194320 | tf_op jit(solution)/shard_map/all_gather | solution.py:177
  50.8 5.8 %copy-done.1 = bf16[513,128,128]{2,1,0:T(8,128)(2,1)S(1)} copy-done((bf16[513,128,128]{2,1,0:T(8,128)(2,1)S(1)}, bf16[513,128,128]{2,1,0:T(8,128)(2,1)}, u32[]{:S(2)}) %copy-start.1) | copy-done | bytes 16810008
  56.6 2.2 copy-done.4
  58.8 4.5 %spread_forward.1 = bf16[32,128,256]{2,1,0:T(8,128)(2,1)S(1)} custom-call(s32[1]{0:T(128)} %bitcast.2.pairs_ref, s32[544]{0:T(1024)S(1)} %broadcast_add_fusion.1.tile_ref, s32[544]{0:T(1024)S(1)} %get-tuple-element.19.pick_ref, s32[544]{0:T(1024)S(1)} %get-tuple-element.18.place_ref, bf16[513,128,128]{2,1,0:T(8,128)(2,1)S(1)} %copy-done.1, ...), custom_call_target="tpu_custom_call" | custom-call | flops 4303355904 | bytes 21004288 | tf_op jit(solution)/shard_map/spread_forward/pallas_call | solution.py:93
  63.3 39.3 %all_to_all.20.parts_ref = bf16[8,512,256]{2,1,0:T(8,128)(2,1)S(1)} all-to-all(bf16[8,512,256]{2,1,0:T(8,128)(2,1)S(1)} %bitcast.16), channel_id=1, replica_groups=mesh['dom'=16,'rep'=8] {'rep'}, dimensions={0} | all-to-all | bytes 4194304 | tf_op jit(solution)/shard_map/all_to_all | solution.py:192
  102.6 1.4 middle.1
  104.0 1.4 copy-done.5
  105.4 3.6 %all-to-all-start.1 = ((bf16[8,576,256]{2,1,0:T(8,128)(2,1)}), bf16[8,576,256]{2,1,0:T(8,128)(2,1)S(1)}, u32[]{:S(2)}, u32[]{:S(2)}) async-start(bf16[8,576,256]{2,1,0:T(8,128)(2,1)} %copy-done.5), calls=%async_computation.1 | async-start | bytes 4718592 | tf_op jit(solution)/shard_map/all_to_all | solution.py:202
  109.0 0.6 select_reduce_fusion
  109.6 30.8 %all-to-all-done.1 = bf16[8,576,256]{2,1,0:T(8,128)(2,1)S(1)} async-done(((bf16[8,576,256]{2,1,0:T(8,128)(2,1)}), bf16[8,576,256]{2,1,0:T(8,128)(2,1)S(1)}, u32[]{:S(2)}, u32[]{:S(2)}) %all-to-all-start.1) | async-done | bytes 2359328 | tf_op jit(solution)/shard_map/all_to_all | solution.py:202
  140.4 5.8 %copy-done.2 = bf16[513,128,128]{2,1,0:T(8,128)(2,1)S(1)} copy-done((bf16[513,128,128]{2,1,0:T(8,128)(2,1)S(1)}, bf16[513,128,128]{2,1,0:T(8,128)(2,1)}, u32[]{:S(2)}) %copy-start.2) | copy-done | bytes 16810008
  146.2 5.5 %spread_back.1 = (bf16[32,128,256]{2,1,0:T(8,128)(2,1)S(1)}, bf16[32,128,256]{2,1,0:T(8,128)(2,1)S(1)}) custom-call(s32[1]{0:T(128)} %bitcast.6.pairs_ref, s32[576]{0:T(1024)S(1)} %broadcast_add_fusion.tile_ref, s32[576]{0:T(1024)S(1)} %get-tuple-element.16.pick_ref, s32[576]{0:T(1024)S(1)} %get-tuple-element.15.place_ref, ...), custom_call_target="tpu_custom_call" | custom-call | flops 4303355904 | bytes 19169280 | tf_op jit(solution)/shard_map/spread_back/pallas_call | solution.py:93
  151.7 6.2 %collective-permute-start = (bf16[8,512,256]{2,1,0:T(8,128)(2,1)S(1)}, bf16[8,512,256]{2,1,0:T(8,128)(2,1)S(1)}, u32[]{:S(2)}, u32[]{:S(2)}) collective-permute-start(bf16[8,512,256]{2,1,0:T(8,128)(2,1)S(1)} %bitcast.18), channel_id=1, source_target_pairs={{0,8},{8,0},{16,24},{24,16},{32,40},{40,32},{48,56},{56,48},{64,72... | collective-permute-start | bytes 6291464 | tf_op jit(solution)/shard_map/ppermute | solution.py:211
  158.1 3.7 %collective-permute-done.1 = f32[32,256]{1,0:T(8,128)S(1)} collective-permute-done((f32[32,256]{1,0:T(8,128)S(1)}, f32[32,256]{1,0:T(8,128)S(1)}, u32[]{:S(2)}, u32[]{:S(2)}) %collective-permute-start.1) | collective-permute-done | bytes 32800 | tf_op jit(solution)/shard_map/ppermute | solution.py:207
  161.8 0.6 join.1
  162.4 31.5 %all_to_all.21.parts_ref = bf16[8,576,256]{2,1,0:T(8,128)(2,1)S(1)} all-to-all(bf16[8,576,256]{2,1,0:T(8,128)(2,1)S(1)} %join.1), channel_id=1, replica_groups={{0,16,32,48,64,80,96,112},{8,24,40,56,72,88,104,120},{1,17,33,49,65,81,..., dimensions={0} | all-to-all | bytes 4718592 | tf_op jit(solution)/shard_map/all_to_all | solution.py:226
  193.9 1.1 last.1
  195.0 17.0 %all_to_all.22 = f32[8,32,256]{2,1,0:T(8,128)S(1)} all-to-all(f32[8,32,256]{2,1,0:T(8,128)S(1)} %get-tuple-element.14), channel_id=1, replica_groups=mesh['dom'=16,'rep'=8] {'rep'}, dimensions={0} | all-to-all | bytes 524288 | tf_op jit(solution)/shard_map/all_to_all | solution.py:236
  212.0 0.7 copy.12
  (28 shorter events, 0.5 us)
Async XLA Ops:
  7.2 43.7 %all-gather.2.cloned.1.call-start = ((), (), s32[]{:S(2)}) async-start(), calls=%async_computation.4 | async-start | bytes 4456448 | tf_op jit(solution)/shard_map/all_gather | solution.py:177
  8.6 5.8 %copy-start.3 = (bf16[1,1,512,128,128]{4,3,2,1,0:T(8,128)(2,1)S(1)}, bf16[1,1,512,128,128]{4,3,2,1,0:T(8,128)(2,1)}, u32[]{:S(2)}) copy-start(bf16[1,1,512,128,128]{4,3,2,1,0:T(8,128)(2,1)} %param.12) | copy-start | bytes 50331652
  14.3 7.0 %copy-start.9 = (s32[1,1,512]{2,1,0:T(1,128)S(1)}, s32[1,1,512]{2,1,0:T(1,128)}, u32[]{:S(2)}) copy-start(s32[1,1,512]{2,1,0:T(1,128)} %param.11) | copy-start | bytes 6148
  14.3 8.2 %copy-start.8 = (s32[1,1,512]{2,1,0:T(1,128)S(1)}, s32[1,1,512]{2,1,0:T(1,128)}, u32[]{:S(2)}) copy-start(s32[1,1,512]{2,1,0:T(1,128)} %param.10) | copy-start | bytes 6148
  15.5 5.7 %copy-start = (bf16[513,128,128]{2,1,0:T(8,128)(2,1)}, bf16[513,128,128]{2,1,0:T(8,128)(2,1)S(1)}, u32[]{:S(2)}) copy-start(bf16[513,128,128]{2,1,0:T(8,128)(2,1)S(1)} %load_tiles.1.tiles_ref) | copy-start | bytes 50429956
  50.8 5.8 %copy-start.1 = (bf16[513,128,128]{2,1,0:T(8,128)(2,1)S(1)}, bf16[513,128,128]{2,1,0:T(8,128)(2,1)}, u32[]{:S(2)}) copy-start(bf16[513,128,128]{2,1,0:T(8,128)(2,1)} %copy-done) | copy-start | bytes 50429956
  56.6 2.2 copy-start.4
  63.3 39.3 %copy-start.6 = (bf16[256,256]{1,0:T(8,128)(2,1)S(1)}, bf16[256,256]{1,0:T(8,128)(2,1)}, u32[]{:S(2)}) copy-start(bf16[256,256]{1,0:T(8,128)(2,1)} %weight_ref.3) | copy-start | bytes 393220
  63.3 39.3 %copy-start.7 = (bf16[512,256]{1,0:T(8,128)(2,1)S(1)}, bf16[512,256]{1,0:T(8,128)(2,1)}, u32[]{:S(2)}) copy-start(bf16[512,256]{1,0:T(8,128)(2,1)} %cotangent_ref.1) | copy-start | bytes 786436
  104.0 1.4 copy-start.5
  105.4 35.0 %all-to-all-start.1 = ((bf16[8,576,256]{2,1,0:T(8,128)(2,1)}), bf16[8,576,256]{2,1,0:T(8,128)(2,1)S(1)}, u32[]{:S(2)}, u32[]{:S(2)}) async-start(bf16[8,576,256]{2,1,0:T(8,128)(2,1)} %copy-done.5), calls=%async_computation.1 | async-start | bytes 4718592 | tf_op jit(solution)/shard_map/all_to_all | solution.py:202
  140.4 5.8 %copy-start.2 = (bf16[513,128,128]{2,1,0:T(8,128)(2,1)S(1)}, bf16[513,128,128]{2,1,0:T(8,128)(2,1)}, u32[]{:S(2)}) copy-start(bf16[513,128,128]{2,1,0:T(8,128)(2,1)} %copy-done) | copy-start | bytes 50429956
  151.7 10.1 %collective-permute-start = (bf16[8,512,256]{2,1,0:T(8,128)(2,1)S(1)}, bf16[8,512,256]{2,1,0:T(8,128)(2,1)S(1)}, u32[]{:S(2)}, u32[]{:S(2)}) collective-permute-start(bf16[8,512,256]{2,1,0:T(8,128)(2,1)S(1)} %bitcast.18), channel_id=1, source_target_pairs={{0,8},{8,0},{16,24},{24,16},{32,40},{40,32},{48,56},{56,48},{64,72... | collective-permute-start | bytes 6291464 | tf_op jit(solution)/shard_map/ppermute | solution.py:211
  158.0 3.8 %collective-permute-start.1 = (f32[32,256]{1,0:T(8,128)S(1)}, f32[32,256]{1,0:T(8,128)S(1)}, u32[]{:S(2)}, u32[]{:S(2)}) collective-permute-start(f32[32,256]{1,0:T(8,128)S(1)} %slice_add_fusion), channel_id=1, source_target_pairs={{0,8},{8,0},{16,24},{24,16},{32,40},{40,32},{48,56},{56,48},{64,72... | collective-permute-start | bytes 98312 | tf_op jit(solution)/shard_map/ppermute | solution.py:207
Sparse Core Ops, SparseCore 0:
  9.7 41.0 all-gather.1

commit v2 on v1

v2 whole, which is shorter than its diff:
```python
import functools

import jax
import jax.numpy as jnp
from jax import lax
from jax.experimental import pallas as pl
from jax.experimental.pallas import tpu as pltpu
from jax.sharding import PartitionSpec as P

BLOCK = 128
UNROLL = 16
SCOPE = 32 << 20


def pair_plan(key, place, pick, count, keys):
    slots = place.shape[0]
    slot = jnp.arange(slots, dtype=jnp.int32)
    live = slot < count
    key = jnp.where(live, key, keys)
    earlier = (key[:, None] == key[None, :]) & (slot[None, :] < slot[:, None])
    rank = jnp.sum(earlier, axis=1, dtype=jnp.int32)
    block = jnp.arange(keys, dtype=jnp.int32)
    per_block = jnp.sum(key[None, :] == block[:, None], axis=1, dtype=jnp.int32)
    pairs = (per_block + 1) // 2
    late = block >= keys // 2
    turns_first = (jnp.sum(jnp.where(late, 0, pairs)) + UNROLL - 1) // UNROLL
    turns_second = (jnp.sum(jnp.where(late, pairs, 0)) + UNROLL - 1) // UNROLL
    before = (block[None, :] < block[:, None]) & (late[None, :] == late[:, None])
    before = jnp.sum(jnp.where(before, pairs[None, :], 0), axis=1, dtype=jnp.int32)
    before += jnp.where(late, turns_first * UNROLL, 0)
    first = jnp.sum(jnp.where(key[:, None] == block[None, :], before[None, :], 0), axis=1, dtype=jnp.int32)
    position = jnp.where(live, 2 * first + rank, -1)
    half = jnp.arange(((slots + keys) // (2 * UNROLL) + 2) * UNROLL * 2, dtype=jnp.int32)
    hit = half[:, None] == position[None, :]
    tile = jnp.sum(jnp.where(hit, slot[None, :] - slots, 0), axis=1, dtype=jnp.int32) + slots
    picked = jnp.sum(jnp.where(hit, pick[None, :], 0), axis=1, dtype=jnp.int32)
    placed = jnp.sum(jnp.where(hit, place[None, :], 0), axis=1, dtype=jnp.int32)
    return jnp.stack([turns_first, turns_second]), tile, picked, placed


def spread_kernel(flipped, sources, turns_ref, tile_ref, pick_ref, place_ref, tiles_ref, *refs):
    source_refs, out_refs = refs[:sources], refs[sources:-3]
    total_ref, held_ref, sems = refs[-3:]
    slots = tiles_ref.shape[0]
    wide = 2 * UNROLL
    middle = turns_ref[0]
    stop = middle + turns_ref[1]

    @pl.loop(0, stop)
    def _(turn):
        for step in range(wide):
            slot = turn * wide + step
            tile = jnp.minimum(tile_ref[slot], slots - 1)
            pltpu.make_async_copy(tiles_ref.at[tile], held_ref.at[slot], sems.at[turn]).start()

    total_ref[...] = jnp.zeros_like(total_ref)

    def tile_of(slot):
        return held_ref[slot] * (tile_ref[slot] < slots).astype(jnp.bfloat16)

    def add_turns(start, end, source_ref):
        def rows_of(slot):
            return source_ref[pl.ds(pl.multiple_of(pick_ref[slot] * BLOCK, BLOCK), BLOCK), :]

        @pl.loop(start, end)
        def _(turn):
            window = pl.ds(turn * wide, wide)
            pltpu.make_async_copy(tiles_ref.at[pl.ds(0, wide)], held_ref.at[window], sems.at[turn]).wait()
            for step in range(UNROLL):
                first = turn * wide + 2 * step
                rows = jnp.concatenate([rows_of(first), rows_of(first + 1)], axis=0)
                tiles = [tile_of(first), tile_of(first + 1)]
                if flipped:
                    product = lax.dot_general(
                        jnp.concatenate(tiles, axis=0),
                        rows,
                        (((0,), (0,)), ((), ())),
                        preferred_element_type=jnp.float32,
                    )
                else:
                    product = jnp.dot(jnp.concatenate(tiles, axis=1), rows, preferred_element_type=jnp.float32)
                total_ref[place_ref[first]] += product

    if sources == 1:
        add_turns(0, stop, source_refs[0])
    else:
        add_turns(0, middle, source_refs[0])
        add_turns(middle, stop, source_refs[1])
    part = total_ref.shape[0] // len(out_refs)
    for i, out_ref in enumerate(out_refs):
        out_ref[...] = total_ref[i * part : (i + 1) * part].astype(out_ref.dtype)


def spread(plan, tiles, sources, places, out_types, flipped):
    width = sources[0].shape[1]
    halves = plan[1].shape[0]
    in_vmem = pl.BlockSpec(memory_space=pltpu.VMEM)
    part = places // len(out_types)
    return pl.pallas_call(
        functools.partial(spread_kernel, flipped, len(sources)),
        out_shape=[jax.ShapeDtypeStruct((part, BLOCK, width), out_type) for out_type in out_types],
        in_specs=[pl.BlockSpec(memory_space=pltpu.SMEM)] * 4
        + [pl.BlockSpec(memory_space=pltpu.HBM)]
        + [in_vmem] * len(sources),
        out_specs=[in_vmem] * len(out_types),
        scratch_shapes=[
            pltpu.VMEM((places, BLOCK, width), jnp.float32),
            pltpu.VMEM((halves, BLOCK, BLOCK), tiles.dtype),
            pltpu.SemaphoreType.DMA((halves // (2 * UNROLL),)),
        ],
        compiler_params=pltpu.CompilerParams(vmem_limit_bytes=SCOPE),
        cost_estimate=pl.CostEstimate(
            flops=2 * tiles.size * width, bytes_accessed=2 * (tiles.size + len(sources) * sources[0].size), transcendentals=0
        ),
        name="spread_back" if flipped else "spread_forward",
    )(*plan, tiles, *sources)


def split(value):
    high = value.astype(jnp.bfloat16)
    return high, (value - high.astype(jnp.float32)).astype(jnp.bfloat16)


def middle_kernel(parts_ref, weight_ref, cotangent_ref, out_ref, send_ref, term_ref):
    members = parts_ref.shape[0]
    mixed = parts_ref[0].astype(jnp.float32)
    for member in range(1, members):
        mixed += parts_ref[member].astype(jnp.float32)
    high, low = split(mixed)
    weight = weight_ref[...]
    summed = jnp.dot(high, weight, preferred_element_type=jnp.float32)
    summed += jnp.dot(low, weight, preferred_element_type=jnp.float32)
    sig = jax.nn.sigmoid(summed)
    out_ref[...] = (summed * sig).astype(out_ref.dtype)
    slope = sig * (1.0 + summed * (1.0 - sig))
    grad = (cotangent_ref[...].astype(jnp.float32) * slope).astype(jnp.bfloat16)
    across = (((0,), (0,)), ((), ()))
    term = lax.dot_general(high, grad, across, preferred_element_type=jnp.float32)
    term += lax.dot_general(low, grad, across, preferred_element_type=jnp.float32)
    term_ref[...] = term
    for member in range(members):
        send_ref[member] = grad


def join_kernel(own_ref, other_ref, term_ref, send_ref):
    rows = own_ref.shape[1]
    share = term_ref.shape[0]
    send_ref[0, :rows, :] = (own_ref[0] + other_ref[0].astype(jnp.float32)).astype(jnp.bfloat16)
    high, low = split(term_ref[...])
    send_ref[0, rows : rows + share, :] = high
    send_ref[0, rows + share :, :] = low


def last_kernel(parts_ref, weight_ref, out_ref, term_ref):
    members = parts_ref.shape[0]
    rows = out_ref.shape[0]
    share = term_ref.shape[0] // members
    total = parts_ref[0, :rows].astype(jnp.float32)
    for member in range(1, members):
        total += parts_ref[member, :rows].astype(jnp.float32)
    grad = total.astype(jnp.bfloat16)
    out_ref[...] = lax.dot_general(
        grad, weight_ref[...], (((1,), (1,)), ((), ())), preferred_element_type=jnp.float32
    ).astype(out_ref.dtype)
    for member in range(members):
        place = sum(((member >> bit) & 1) * (term_ref.shape[0] >> (bit + 1)) for bit in range(members.bit_length() - 1))
        high = parts_ref[member, rows : rows + share].astype(jnp.float32)
        term_ref[place : place + share, :] = high + parts_ref[member, rows + share :].astype(jnp.float32)


def exchange(value, axis, bit):
    size = lax.axis_size(axis)
    return lax.ppermute(value, axis, [(place, place ^ bit) for place in range(size)])


def halve(value, axis, bit):
    size = value.shape[0] // 2
    upper = (lax.axis_index(axis) & bit) != 0
    low, high = value[:size], value[size:]
    return jnp.where(upper, high, low) + exchange(jnp.where(upper, low, high), axis, bit)


def body(node_features, weight, cotangent, tile_row, tile_col, tile_values, tile_count):
    rows, width = node_features.shape
    dom_size = lax.axis_size("dom")
    rep_size = lax.axis_size("rep")
    slots = tile_row.shape[2]
    own = rows // BLOCK
    chips = dom_size // 2
    share = width // chips
    wide = rows + 2 * share
    params = pltpu.CompilerParams(vmem_limit_bytes=24 << 20)
    row_index = tile_row.reshape(slots)
    col_index = tile_col.reshape(slots)
    count = tile_count.reshape(())
    tiles = pltpu.with_memory_space_constraint(tile_values.reshape(slots, BLOCK, BLOCK), pltpu.HBM)
    parity = lax.axis_index("dom") % 2

    same_core = [list(range(core, dom_size, 2)) for core in range(2)]
    row_blocks = rep_size * own
    col_blocks = chips * own

    owner = col_index // own
    away = (owner + parity) % 2
    col_own = (owner // 2) * own + col_index % own
    forward_plan = pair_plan(
        away * row_blocks + row_index, row_index, col_own, count, 2 * row_blocks
    )
    col_place = away * col_blocks + col_own
    back_plan = pair_plan(col_place, col_place, row_index, count, 2 * col_blocks)

    copies = jnp.broadcast_to(node_features[None], (chips, rows, width))
    near = lax.all_to_all(copies, "dom", 0, 0, axis_index_groups=same_core, tiled=True)
    far = exchange(near, "dom", 1)
    near, far = near.reshape(chips * rows, width), far.reshape(chips * rows, width)
    (partial,) = spread(forward_plan, tiles, [near, far], row_blocks, [jnp.bfloat16], False)
    parts = lax.all_to_all(partial.reshape(rep_size, rows, width), "rep", 0, 0, tiled=True)
    output, grads, term = pl.pallas_call(
        middle_kernel,
        out_shape=(
            jax.ShapeDtypeStruct((rows, width), jnp.bfloat16),
            jax.ShapeDtypeStruct((rep_size, rows, width), jnp.bfloat16),
            jax.ShapeDtypeStruct((width, width), jnp.float32),
        ),
        compiler_params=params,
        name="middle",
    )(parts, weight, cotangent)
    grads = lax.all_to_all(grads, "rep", 0, 0, tiled=True).reshape(rep_size * rows, width)

    term = term + exchange(term, "dom", 1)
    bit = 2
    while bit < dom_size:
        term = halve(term, "dom", bit)
        bit *= 2
    bit = rep_size // 2
    term = term + exchange(term, "rep", bit)
    grads, term = lax.optimization_barrier((grads, term))

    bit //= 2
    term = term + exchange(term, "rep", bit)
    mine, other = spread(
        back_plan, tiles, [grads], 2 * col_blocks, [jnp.float32, jnp.bfloat16], True
    )
    mine, other = mine.reshape(chips, rows, width), other.reshape(chips, rows, width)
    other = exchange(other, "dom", 1)
    while bit > 1:
        bit //= 2
        term = term + exchange(term, "rep", bit)
    joined = pl.pallas_call(
        join_kernel,
        grid=(chips,),
        out_shape=jax.ShapeDtypeStruct((chips, wide, width), jnp.bfloat16),
        in_specs=[
            pl.BlockSpec((1, rows, width), lambda i: (i, 0, 0)),
            pl.BlockSpec((1, rows, width), lambda i: (i, 0, 0)),
            pl.BlockSpec((share, width), lambda i: (0, 0)),
        ],
        out_specs=pl.BlockSpec((1, wide, width), lambda i: (i, 0, 0)),
        compiler_params=params,
        name="join",
    )(mine, other, term)
    back_parts = lax.all_to_all(joined, "dom", 0, 0, axis_index_groups=same_core, tiled=True)
    grad_features, grad_weight = pl.pallas_call(
        last_kernel,
        out_shape=(
            jax.ShapeDtypeStruct((rows, width), jnp.bfloat16),
            jax.ShapeDtypeStruct((width, width), jnp.float32),
        ),
        compiler_params=params,
        name="last",
    )(back_parts, weight)
    return (output, grad_features, grad_weight)


def solution(mesh):
    placed = (
        P(("dom", "rep"), None),
        P(),
        P(("dom", "rep"), None),
        P("dom", "rep", None),
        P("dom", "rep", None),
        P("dom", "rep", None, None, None),
        P("dom", "rep"),
    )
    return jax.shard_map(
        body,
        mesh=mesh,
        in_specs=placed,
        out_specs=(P(("dom", "rep"), None), P(("dom", "rep"), None), P()),
        check_vma=False,
    )
```

time: 222 us -> 179 us (0.81)
  local copies, waits for them, and re-layouts: 27.4 us -> 3.81 us
  starting transfers between devices: 9.97 us -> 26.1 us
  blocking collectives: 87.7 us -> 73.4 us
  waiting for transfers between devices: 61.7 us -> 50.4 us
  between operations: 14.8 us -> 4.15 us
    all_gather x1 -> x0, waiting for transfers between devices: 26.5 us -> none  [body(): gathered = lax.all_gather(node_features, 'dom', axis=0, tiled=True)]
    unnamed x21 -> x10, local copies, waits for them, and re-layouts: 27.4 us -> 1.37 us
    ppermute x2 -> x9, waiting for transfers between devices: 3.68 us -> 28.6 us  [exchange(): lax.ppermute(value, axis, [(place, place ^ bit) for place in range(size)])]
    all_to_all x1 -> x0, blocking collectives: 17 us -> none  [body(): lax.all_to_all(term_out, 'rep', 0, 0, tiled=True).reshape(width, width)]
    ppermute x2 -> x9, starting transfers between devices: 6.31 us -> 15.5 us  [exchange(): lax.ppermute(value, axis, [(place, place ^ bit) for place in range(size)])]
    all_to_all x1 -> x2, waiting for transfers between devices: 30.8 us -> 21.9 us  [the longest x1 21.9 us: body(): lax.all_to_all(copies, 'dom', 0, 0, axis_index_groups=same_core, tiled=True)]
    all_to_all x1 -> x2, starting transfers between devices: 3.61 us -> 10.6 us  [the longest x1 7.01 us: body(): lax.all_to_all(copies, 'dom', 0, 0, axis_index_groups=same_core, tiled=True)]
    broadcast_in_dim x0 -> x1, local copies, waits for them, and re-layouts: none -> 2.44 us  [body(): copies = jnp.broadcast_to(node_features[None], (chips, rows, width))]
  transfers between devices with their start and end apart: 4 -> 11, of which waited for: 3 -> 8; matrix products, arithmetic and copies ran while one was open for 2% -> 2% of each run, Pallas kernels for 1% -> 0%
where the time goes in v2:
time: 179 us; the launch traced here: 177 us
  blocking collectives  73.4 us (41%)
  waiting for transfers between devices  50.4 us (28%)
  starting transfers between devices  26.1 us (15%)
  Pallas kernels  15.3 us (9%)
  between operations  4.15 us (2%)
  other arithmetic  3.97 us (2%)
  local copies, waits for them, and re-layouts  3.81 us (2%)
    all_to_all x1, blocking collectives, body(): lax.all_to_all(partial.reshape(rep_size, rows, width), 'rep', 0, 0, tiled...  40.3 us
    all_to_all x1, blocking collectives, body(): lax.all_to_all(joined, 'dom', 0, 0, axis_index_groups=same_core, tiled=True)  33.1 us
    ppermute x9, waiting for transfers between devices, exchange(): lax.ppermute(value, axis, [(place, place ^ bit) for place in range(size)])  28.6 us
    all_to_all x1, waiting for transfers between devices, body(): lax.all_to_all(copies, 'dom', 0, 0, axis_index_groups=same_core, tiled=True)  21.9 us
    ppermute x9, starting transfers between devices, exchange(): lax.ppermute(value, axis, [(place, place ^ bit) for place in range(size)])  15.5 us
    pallas_call x2, Pallas kernels, spread(): pl.pallas_call(functools.partial(spread_kernel, flipped, len(sources)), o...  12.2 us
    all_to_all x1, starting transfers between devices, body(): lax.all_to_all(copies, 'dom', 0, 0, axis_index_groups=same_core, tiled=True)  7.01 us
    all_to_all x1, starting transfers between devices, body(): lax.all_to_all(grads, 'rep', 0, 0, tiled=True)  3.6 us
  transfers between devices with their start and end apart: 11, of which 8 were waited for; matrix products, arithmetic and copies ran while one was open for 2% of the time, Pallas kernels for 0%

profile of v2, /device:TPU:1, one launch (start us, length us, event | category | flops | bytes accessed | tf_op | source)
XLA Modules:
  0.0 177.1 jit_solution(4753288132748515771)
XLA Ops:
  0.6 2.4 %broadcast_in_dim.154 = bf16[8,512,256]{2,1,0:T(8,128)(2,1)} broadcast(bf16[512,256]{1,0:T(8,128)(2,1)} %param.7), dimensions={1,2} | broadcast | bytes 2359296 | tf_op jit(solution)/shard_map/broadcast_in_dim | solution.py:212
  3.1 7.0 %all-to-all-start = ((bf16[8,512,256]{2,1,0:T(8,128)(2,1)}), bf16[8,512,256]{2,1,0:T(8,128)(2,1)S(1)}, u32[]{:S(2)}, u32[]{:S(2)}) async-start(bf16[8,512,256]{2,1,0:T(8,128)(2,1)} %broadcast_in_dim.154), calls=%async_computation | async-start | bytes 4194304 | tf_op jit(solution)/shard_map/all_to_all | solution.py:213
  10.9 0.7 select_reduce_fusion.11
  12.3 0.7 select_reduce_fusion.13
  14.4 21.9 %all-to-all-done = bf16[8,512,256]{2,1,0:T(8,128)(2,1)S(1)} async-done(((bf16[8,512,256]{2,1,0:T(8,128)(2,1)}), bf16[8,512,256]{2,1,0:T(8,128)(2,1)S(1)}, u32[]{:S(2)}, u32[]{:S(2)}) %all-to-all-start) | async-done | bytes 2097184 | tf_op jit(solution)/shard_map/all_to_all | solution.py:213
  36.2 0.8 collective-permute-start
  37.2 0.2 select_reduce_fusion.8
  37.6 0.2 convert_reduce_fusion.1
  37.8 0.3 convert_reduce_fusion
  38.1 1.2 select_reduce_fusion
  39.3 1.6 collective-permute-done
  40.9 5.4 %spread_forward.1 = bf16[32,128,256]{2,1,0:T(8,128)(2,1)S(1)} custom-call(s32[2]{0:T(128)S(1)} %pad_add_fusion.turns_ref, s32[640]{0:T(1024)S(1)} %broadcast_add_fusion.1.tile_ref, s32[640]{0:T(1024)S(1)} %get-tuple-element.24.pick_ref, s32[640]{0:T(1024)S(1)} %get-tuple-element.23.place_ref, bf16[512,128,128]{2,1,0:T(8,128)(2,1)} %bitcast.23, ...), custom_call_target="tpu_custom_call" | custom-call | flops 4294967296 | bytes 20971520 | tf_op jit(solution)/shard_map/spread_forward/pallas_call | solution.py:99
  46.3 40.3 %all_to_all.20.parts_ref = bf16[8,512,256]{2,1,0:T(8,128)(2,1)S(1)} all-to-all(bf16[8,512,256]{2,1,0:T(8,128)(2,1)S(1)} %bitcast.18), channel_id=1, replica_groups=mesh['dom'=16,'rep'=8] {'rep'}, dimensions={0} | all-to-all | bytes 4194304 | tf_op jit(solution)/shard_map/all_to_all | solution.py:217
  86.7 1.4 middle.1
  88.1 1.3 copy-done
  89.4 1.2 collective-permute-start.1
  90.6 3.6 %all-to-all-start.2 = ((bf16[8,512,256]{2,1,0:T(8,128)(2,1)}), bf16[8,512,256]{2,1,0:T(8,128)(2,1)S(1)}, u32[]{:S(2)}, u32[]{:S(2)}) async-start(bf16[8,512,256]{2,1,0:T(8,128)(2,1)} %copy-done), calls=%async_computation.2 | async-start | bytes 4194304 | tf_op jit(solution)/shard_map/all_to_all | solution.py:228
  94.4 5.1 %collective-permute-done.2 = f32[128,256]{1,0:T(8,128)S(1)} collective-permute-done((f32[128,256]{1,0:T(8,128)S(1)}, f32[128,256]{1,0:T(8,128)S(1)}, u32[]{:S(2)}, u32[]{:S(2)}) %collective-permute-start.2) | collective-permute-done | bytes 131104 | tf_op jit(solution)/shard_map/ppermute | solution.py:173
  99.6 0.8 collective-permute-start.3
  100.4 4.2 %collective-permute-done.3 = f32[64,256]{1,0:T(8,128)S(1)} collective-permute-done((f32[64,256]{1,0:T(8,128)S(1)}, f32[64,256]{1,0:T(8,128)S(1)}, u32[]{:S(2)}, u32[]{:S(2)}) %collective-permute-start.3) | collective-permute-done | bytes 65568 | tf_op jit(solution)/shard_map/ppermute | solution.py:173
  105.4 8.0 %collective-permute-done.4 = f32[32,256]{1,0:T(8,128)S(1)} collective-permute-done((f32[32,256]{1,0:T(8,128)S(1)}, f32[32,256]{1,0:T(8,128)S(1)}, u32[]{:S(2)}, u32[]{:S(2)}) %collective-permute-start.4) | collective-permute-done | bytes 32800 | tf_op jit(solution)/shard_map/ppermute | solution.py:173
  113.4 3.3 %collective-permute-start.5 = (f32[32,256]{1,0:T(8,128)S(1)}, f32[32,256]{1,0:T(8,128)S(1)}, u32[]{:S(2)}, u32[]{:S(2)}) collective-permute-start(f32[32,256]{1,0:T(8,128)S(1)} %select_add_fusion.2), channel_id=1, source_target_pairs={{0,4},{1,5},{2,6},{3,7},{4,0},{5,1},{6,2},{7,3},{8,12},{9,13},{10,... | collective-permute-start | bytes 98312 | tf_op jit(solution)/shard_map/ppermute | solution.py:173
  116.7 7.1 %collective-permute-done.5 = f32[32,256]{1,0:T(8,128)S(1)} collective-permute-done((f32[32,256]{1,0:T(8,128)S(1)}, f32[32,256]{1,0:T(8,128)S(1)}, u32[]{:S(2)}, u32[]{:S(2)}) %collective-permute-start.5) | collective-permute-done | bytes 32800 | tf_op jit(solution)/shard_map/ppermute | solution.py:173
  123.8 6.8 %spread_back.1 = (f32[32,128,256]{2,1,0:T(8,128)S(1)}, bf16[32,128,256]{2,1,0:T(8,128)(2,1)S(1)}) custom-call(s32[2]{0:T(128)S(1)} %pad_add_fusion.1.turns_ref, s32[640]{0:T(1024)S(1)} %broadcast_add_fusion.tile_ref, s32[640]{0:T(1024)S(1)} %get-tuple-element.22.pick_ref, s32[640]{0:T(1024)S(1)} %get-tuple-element.21.place_ref, ...), custom_call_target="tpu_custom_call" | custom-call | flops 4294967296 | bytes 18874368 | tf_op jit(solution)/shard_map/spread_back/pallas_call | solution.py:99
  130.6 3.4 %collective-permute-start.6 = (bf16[8,512,256]{2,1,0:T(8,128)(2,1)S(1)}, bf16[8,512,256]{2,1,0:T(8,128)(2,1)S(1)}, u32[]{:S(2)}, u32[]{:S(2)}) collective-permute-start(bf16[8,512,256]{2,1,0:T(8,128)(2,1)S(1)} %bitcast.22), channel_id=1, source_target_pairs={{0,8},{8,0},{16,24},{24,16},{32,40},{40,32},{48,56},{56,48},{64,72... | collective-permute-start | bytes 6291464 | tf_op jit(solution)/shard_map/ppermute | solution.py:173
  134.0 3.0 %collective-permute-start.7 = (f32[32,256]{1,0:T(8,128)S(1)}, f32[32,256]{1,0:T(8,128)S(1)}, u32[]{:S(2)}, u32[]{:S(2)}) collective-permute-start(f32[32,256]{1,0:T(8,128)S(1)} %add.271), channel_id=1, source_target_pairs={{0,2},{1,3},{2,0},{3,1},{4,6},{5,7},{6,4},{7,5},{8,10},{9,11},{10,... | collective-permute-start | bytes 98312 | tf_op jit(solution)/shard_map/ppermute | solution.py:173
  137.0 1.3 collective-permute-done.7
  138.3 2.7 %collective-permute-start.8 = (f32[32,256]{1,0:T(8,128)S(1)}, f32[32,256]{1,0:T(8,128)S(1)}, u32[]{:S(2)}, u32[]{:S(2)}) collective-permute-start(f32[32,256]{1,0:T(8,128)S(1)} %add.272), channel_id=1, source_target_pairs={{0,1},{1,0},{2,3},{3,2},{4,5},{5,4},{6,7},{7,6},{8,9},{9,8},{10,11... | collective-permute-start | bytes 98312 | tf_op jit(solution)/shard_map/ppermute | solution.py:173
  141.0 1.3 collective-permute-done.8
  142.4 0.5 join.1
  142.9 33.1 %all_to_all.21.parts_ref = bf16[8,576,256]{2,1,0:T(8,128)(2,1)S(1)} all-to-all(bf16[8,576,256]{2,1,0:T(8,128)(2,1)S(1)} %join.1), channel_id=1, replica_groups={{0,16,32,48,64,80,96,112},{8,24,40,56,72,88,104,120},{1,17,33,49,65,81,..., dimensions={0} | all-to-all | bytes 4718592 | tf_op jit(solution)/shard_map/all_to_all | solution.py:262
  176.0 1.1 last.1
  (39 shorter events, 1.0 us)
Async XLA Ops:
  3.1 7.7 %copy-start.4 = (s32[1,1,512]{2,1,0:T(1,128)S(1)}, s32[1,1,512]{2,1,0:T(1,128)}, u32[]{:S(2)}) copy-start(s32[1,1,512]{2,1,0:T(1,128)} %param.11) | copy-start | bytes 6148
  3.1 9.1 %copy-start.3 = (s32[1,1,512]{2,1,0:T(1,128)S(1)}, s32[1,1,512]{2,1,0:T(1,128)}, u32[]{:S(2)}) copy-start(s32[1,1,512]{2,1,0:T(1,128)} %param.10) | copy-start | bytes 6148
  3.1 33.2 %all-to-all-start = ((bf16[8,512,256]{2,1,0:T(8,128)(2,1)}), bf16[8,512,256]{2,1,0:T(8,128)(2,1)S(1)}, u32[]{:S(2)}, u32[]{:S(2)}) async-start(bf16[8,512,256]{2,1,0:T(8,128)(2,1)} %broadcast_in_dim.154), calls=%async_computation | async-start | bytes 4194304 | tf_op jit(solution)/shard_map/all_to_all | solution.py:213
  36.2 4.6 %collective-permute-start = (bf16[8,512,256]{2,1,0:T(8,128)(2,1)S(1)}, bf16[8,512,256]{2,1,0:T(8,128)(2,1)S(1)}, u32[]{:S(2)}, u32[]{:S(2)}) collective-permute-start(bf16[8,512,256]{2,1,0:T(8,128)(2,1)S(1)} %all-to-all-done), channel_id=1, source_target_pairs={{0,8},{8,0},{16,24},{24,16},{32,40},{40,32},{48,56},{56,48},{64,72... | collective-permute-start | bytes 6291464 | tf_op jit(solution)/shard_map/ppermute | solution.py:173
  46.3 40.3 %copy-start.1 = (bf16[256,256]{1,0:T(8,128)(2,1)S(1)}, bf16[256,256]{1,0:T(8,128)(2,1)}, u32[]{:S(2)}) copy-start(bf16[256,256]{1,0:T(8,128)(2,1)} %weight_ref.3) | copy-start | bytes 393220
  46.3 40.3 %copy-start.2 = (bf16[512,256]{1,0:T(8,128)(2,1)S(1)}, bf16[512,256]{1,0:T(8,128)(2,1)}, u32[]{:S(2)}) copy-start(bf16[512,256]{1,0:T(8,128)(2,1)} %cotangent_ref.1) | copy-start | bytes 786436
  88.1 1.4 copy-start
  89.4 4.9 %collective-permute-start.1 = (f32[256,256]{1,0:T(8,128)S(1)}, f32[256,256]{1,0:T(8,128)S(1)}, u32[]{:S(2)}, u32[]{:S(2)}) collective-permute-start(f32[256,256]{1,0:T(8,128)S(1)} %get-tuple-element.14), channel_id=1, source_target_pairs={{0,8},{8,0},{16,24},{24,16},{32,40},{40,32},{48,56},{56,48},{64,72... | collective-permute-start | bytes 786440 | tf_op jit(solution)/shard_map/ppermute | solution.py:173
  90.6 33.2 %all-to-all-start.2 = ((bf16[8,512,256]{2,1,0:T(8,128)(2,1)}), bf16[8,512,256]{2,1,0:T(8,128)(2,1)S(1)}, u32[]{:S(2)}, u32[]{:S(2)}) async-start(bf16[8,512,256]{2,1,0:T(8,128)(2,1)} %copy-done), calls=%async_computation.2 | async-start | bytes 4194304 | tf_op jit(solution)/shard_map/all_to_all | solution.py:228
  94.3 5.2 %collective-permute-start.2 = (f32[128,256]{1,0:T(8,128)S(1)}, f32[128,256]{1,0:T(8,128)S(1)}, u32[]{:S(2)}, u32[]{:S(2)}) collective-permute-start(f32[128,256]{1,0:T(8,128)S(1)} %slice_select_fusion), channel_id=1, source_target_pairs={{0,16},{8,24},{16,0},{24,8},{32,48},{40,56},{48,32},{56,40},{64,80... | collective-permute-start | bytes 393224 | tf_op jit(solution)/shard_map/ppermute | solution.py:173
  99.6 5.0 %collective-permute-start.3 = (f32[64,256]{1,0:T(8,128)S(1)}, f32[64,256]{1,0:T(8,128)S(1)}, u32[]{:S(2)}, u32[]{:S(2)}) collective-permute-start(f32[64,256]{1,0:T(8,128)S(1)} %slice_select_fusion.1), channel_id=1, source_target_pairs={{0,32},{8,40},{16,48},{24,56},{32,0},{40,8},{48,16},{56,24},{64,96... | collective-permute-start | bytes 196616 | tf_op jit(solution)/shard_map/ppermute | solution.py:173
  104.6 8.7 %collective-permute-start.4 = (f32[32,256]{1,0:T(8,128)S(1)}, f32[32,256]{1,0:T(8,128)S(1)}, u32[]{:S(2)}, u32[]{:S(2)}) collective-permute-start(f32[32,256]{1,0:T(8,128)S(1)} %slice_select_fusion.2), channel_id=1, source_target_pairs={{0,64},{8,72},{16,80},{24,88},{32,96},{40,104},{48,112},{56,120},{... | collective-permute-start | bytes 98312 | tf_op jit(solution)/shard_map/ppermute | solution.py:173
  113.4 10.4 %collective-permute-start.5 = (f32[32,256]{1,0:T(8,128)S(1)}, f32[32,256]{1,0:T(8,128)S(1)}, u32[]{:S(2)}, u32[]{:S(2)}) collective-permute-start(f32[32,256]{1,0:T(8,128)S(1)} %select_add_fusion.2), channel_id=1, source_target_pairs={{0,4},{1,5},{2,6},{3,7},{4,0},{5,1},{6,2},{7,3},{8,12},{9,13},{10,... | collective-permute-start | bytes 98312 | tf_op jit(solution)/shard_map/ppermute | solution.py:173
  130.6 11.7 %collective-permute-start.6 = (bf16[8,512,256]{2,1,0:T(8,128)(2,1)S(1)}, bf16[8,512,256]{2,1,0:T(8,128)(2,1)S(1)}, u32[]{:S(2)}, u32[]{:S(2)}) collective-permute-start(bf16[8,512,256]{2,1,0:T(8,128)(2,1)S(1)} %bitcast.22), channel_id=1, source_target_pairs={{0,8},{8,0},{16,24},{24,16},{32,40},{40,32},{48,56},{56,48},{64,72... | collective-permute-start | bytes 6291464 | tf_op jit(solution)/shard_map/ppermute | solution.py:173
  134.0 4.3 %collective-permute-start.7 = (f32[32,256]{1,0:T(8,128)S(1)}, f32[32,256]{1,0:T(8,128)S(1)}, u32[]{:S(2)}, u32[]{:S(2)}) collective-permute-start(f32[32,256]{1,0:T(8,128)S(1)} %add.271), channel_id=1, source_target_pairs={{0,2},{1,3},{2,0},{3,1},{4,6},{5,7},{6,4},{7,5},{8,10},{9,11},{10,... | collective-permute-start | bytes 98312 | tf_op jit(solution)/shard_map/ppermute | solution.py:173
  138.3 4.0 %collective-permute-start.8 = (f32[32,256]{1,0:T(8,128)S(1)}, f32[32,256]{1,0:T(8,128)S(1)}, u32[]{:S(2)}, u32[]{:S(2)}) collective-permute-start(f32[32,256]{1,0:T(8,128)S(1)} %add.272), channel_id=1, source_target_pairs={{0,1},{1,0},{2,3},{3,2},{4,5},{5,4},{6,7},{7,6},{8,9},{9,8},{10,11... | collective-permute-start | bytes 98312 | tf_op jit(solution)/shard_map/ppermute | solution.py:173

commit v3 on v2

--- a/solution.py
+++ b/solution.py
@@ -121,7 +121,26 @@
     return high, (value - high.astype(jnp.float32)).astype(jnp.bfloat16)
 
 
-def middle_kernel(parts_ref, weight_ref, cotangent_ref, out_ref, send_ref, term_ref):
+def copies_kernel(value_ref, copies_ref, sems):
+    copies = [pltpu.make_async_copy(value_ref, copies_ref.at[i], sems.at[i]) for i in range(copies_ref.shape[0])]
+    for copy in copies:
+        copy.start()
+    for copy in copies:
+        copy.wait()
+
+
+def copies_of(value, members):
+    return pl.pallas_call(
+        copies_kernel,
+        out_shape=pltpu.HBM((members, *value.shape), value.dtype),
+        in_specs=[pl.BlockSpec(memory_space=pltpu.VMEM)],
+        out_specs=pl.BlockSpec(memory_space=pltpu.HBM),
+        scratch_shapes=[pltpu.SemaphoreType.DMA((members,))],
+        name="copies",
+    )(value)
+
+
+def middle_kernel(parts_ref, weight_ref, cotangent_ref, out_ref, send_ref, term_ref, grad_ref, sems):
     members = parts_ref.shape[0]
     mixed = parts_ref[0].astype(jnp.float32)
     for member in range(1, members):
@@ -131,41 +150,44 @@
     summed = jnp.dot(high, weight, preferred_element_type=jnp.float32)
     summed += jnp.dot(low, weight, preferred_element_type=jnp.float32)
     sig = jax.nn.sigmoid(summed)
-    out_ref[...] = (summed * sig).astype(out_ref.dtype)
     slope = sig * (1.0 + summed * (1.0 - sig))
     grad = (cotangent_ref[...].astype(jnp.float32) * slope).astype(jnp.bfloat16)
+    grad_ref[...] = grad
+    copies = [pltpu.make_async_copy(grad_ref, send_ref.at[i], sems.at[i]) for i in range(members)]
+    for copy in copies:
+        copy.start()
+    out_ref[...] = (summed * sig).astype(out_ref.dtype)
     across = (((0,), (0,)), ((), ()))
     term = lax.dot_general(high, grad, across, preferred_element_type=jnp.float32)
     term += lax.dot_general(low, grad, across, preferred_element_type=jnp.float32)
     term_ref[...] = term
-    for member in range(members):
-        send_ref[member] = grad
+    for copy in copies:
+        copy.wait()
 
 
 def join_kernel(own_ref, other_ref, term_ref, send_ref):
     rows = own_ref.shape[1]
-    share = term_ref.shape[0]
     send_ref[0, :rows, :] = (own_ref[0] + other_ref[0].astype(jnp.float32)).astype(jnp.bfloat16)
-    high, low = split(term_ref[...])
-    send_ref[0, rows : rows + share, :] = high
-    send_ref[0, rows + share :, :] = low
+    send_ref[0, rows:, :] = term_ref[...].astype(jnp.bfloat16)
 
 
 def last_kernel(parts_ref, weight_ref, out_ref, term_ref):
     members = parts_ref.shape[0]
     rows = out_ref.shape[0]
-    share = term_ref.shape[0] // members
-    total = parts_ref[0, :rows].astype(jnp.float32)
+    share = parts_ref.shape[1] - rows
+    pieces = term_ref.shape[0] // share
+    grad = parts_ref[0, :rows].astype(jnp.float32)
     for member in range(1, members):
-        total += parts_ref[member, :rows].astype(jnp.float32)
-    grad = total.astype(jnp.bfloat16)
+        grad += parts_ref[member, :rows].astype(jnp.float32)
     out_ref[...] = lax.dot_general(
-        grad, weight_ref[...], (((1,), (1,)), ((), ())), preferred_element_type=jnp.float32
+        grad.astype(jnp.bfloat16), weight_ref[...], (((1,), (1,)), ((), ())), preferred_element_type=jnp.float32
     ).astype(out_ref.dtype)
-    for member in range(members):
-        place = sum(((member >> bit) & 1) * (term_ref.shape[0] >> (bit + 1)) for bit in range(members.bit_length() - 1))
-        high = parts_ref[member, rows : rows + share].astype(jnp.float32)
-        term_ref[place : place + share, :] = high + parts_ref[member, rows + share :].astype(jnp.float32)
+    for piece in range(pieces):
+        place = sum(((piece >> bit) & 1) * (term_ref.shape[0] >> (bit + 1)) for bit in range(pieces.bit_length() - 1))
+        total = parts_ref[piece, rows:].astype(jnp.float32)
+        for member in range(piece + pieces, members, pieces):
+            total += parts_ref[member, rows:].astype(jnp.float32)
+        term_ref[place : place + share, :] = total
 
 
 def exchange(value, axis, bit):
@@ -187,8 +209,8 @@
     slots = tile_row.shape[2]
     own = rows // BLOCK
     chips = dom_size // 2
-    share = width // chips
-    wide = rows + 2 * share
+    pieces = chips // 2
+    wide = rows + width // pieces
     params = pltpu.CompilerParams(vmem_limit_bytes=24 << 20)
     row_index = tile_row.reshape(slots)
     col_index = tile_col.reshape(slots)
@@ -209,43 +231,41 @@
     col_place = away * col_blocks + col_own
     back_plan = pair_plan(col_place, col_place, row_index, count, 2 * col_blocks)
 
-    copies = jnp.broadcast_to(node_features[None], (chips, rows, width))
-    near = lax.all_to_all(copies, "dom", 0, 0, axis_index_groups=same_core, tiled=True)
+    near = lax.all_to_all(copies_of(node_features, chips), "dom", 0, 0, axis_index_groups=same_core, tiled=True)
     far = exchange(near, "dom", 1)
     near, far = near.reshape(chips * rows, width), far.reshape(chips * rows, width)
     (partial,) = spread(forward_plan, tiles, [near, far], row_blocks, [jnp.bfloat16], False)
     parts = lax.all_to_all(partial.reshape(rep_size, rows, width), "rep", 0, 0, tiled=True)
+    in_vmem = pl.BlockSpec(memory_space=pltpu.VMEM)
     output, grads, term = pl.pallas_call(
         middle_kernel,
         out_shape=(
             jax.ShapeDtypeStruct((rows, width), jnp.bfloat16),
-            jax.ShapeDtypeStruct((rep_size, rows, width), jnp.bfloat16),
+            pltpu.HBM((rep_size, rows, width), jnp.bfloat16),
             jax.ShapeDtypeStruct((width, width), jnp.float32),
         ),
+        in_specs=[in_vmem] * 3,
+        out_specs=(in_vmem, pl.BlockSpec(memory_space=pltpu.HBM), in_vmem),
+        scratch_shapes=[pltpu.VMEM((rows, width), jnp.bfloat16), pltpu.SemaphoreType.DMA((rep_size,))],
         compiler_params=params,
         name="middle",
     )(parts, weight, cotangent)
     grads = lax.all_to_all(grads, "rep", 0, 0, tiled=True).reshape(rep_size * rows, width)
 
-    term = term + exchange(term, "dom", 1)
     bit = 2
-    while bit < dom_size:
+    while bit <= pieces:
         term = halve(term, "dom", bit)
         bit *= 2
-    bit = rep_size // 2
-    term = term + exchange(term, "rep", bit)
+    term = term + exchange(term, "dom", 1)
+    term = term + exchange(term, "rep", rep_size // 2)
     grads, term = lax.optimization_barrier((grads, term))
 
-    bit //= 2
-    term = term + exchange(term, "rep", bit)
     mine, other = spread(
         back_plan, tiles, [grads], 2 * col_blocks, [jnp.float32, jnp.bfloat16], True
     )
     mine, other = mine.reshape(chips, rows, width), other.reshape(chips, rows, width)
     other = exchange(other, "dom", 1)
-    while bit > 1:
-        bit //= 2
-        term = term + exchange(term, "rep", bit)
+    term = (term + exchange(term, "rep", 2)) + (exchange(term, "rep", 1) + exchange(term, "rep", 3))
     joined = pl.pallas_call(
         join_kernel,
         grid=(chips,),
@@ -253,7 +273,7 @@
         in_specs=[
             pl.BlockSpec((1, rows, width), lambda i: (i, 0, 0)),
             pl.BlockSpec((1, rows, width), lambda i: (i, 0, 0)),
-            pl.BlockSpec((share, width), lambda i: (0, 0)),
+            pl.BlockSpec((width // pieces, width), lambda i: (0, 0)),
         ],
         out_specs=pl.BlockSpec((1, wide, width), lambda i: (i, 0, 0)),
         compiler_params=params,

time: 179 us -> 178 us (level)
  waiting for transfers between devices: 50.4 us -> 39.9 us
  Pallas kernels: 15.3 us -> 22.9 us
  starting transfers between devices: 26.1 us -> 33.5 us
  local copies, waits for them, and re-layouts: 3.81 us -> 0.03 us
  blocking collectives: 73.4 us -> 70.7 us
    ppermute x9, waiting for transfers between devices: 28.6 us -> 18 us  [exchange(): lax.ppermute(value, axis, [(place, place ^ bit) for place in range(size)])]
    all_to_all x1, blocking collectives: 40.3 us -> 31.4 us  [body(): lax.all_to_all(partial.reshape(rep_size, rows, width), 'rep', 0, 0, tiled...]
    ppermute x9, starting transfers between devices: 15.5 us -> 23 us  [exchange(): lax.ppermute(value, axis, [(place, place ^ bit) for place in range(size)])]
    all_to_all x1, blocking collectives: 33.1 us -> 39.3 us  [body(): lax.all_to_all(joined, 'dom', 0, 0, axis_index_groups=same_core, tiled=True)]
    pallas_call x2, Pallas kernels: 12.2 us -> 16.1 us  [spread(): pl.pallas_call(functools.partial(spread_kernel, flipped, len(sources)), o...]
    broadcast_in_dim x1 -> x0, local copies, waits for them, and re-layouts: 2.44 us -> none  [body(): copies = jnp.broadcast_to(node_features[None], (chips, rows, width))]
    pallas_call x0 -> x1, Pallas kernels: none -> 2.37 us  [copies_of(): pl.pallas_call(copies_kernel, out_shape=pltpu.HBM((members, *value.shape)...]
where the time goes in v3:
time: 178 us; the launch traced here: 175 us
  blocking collectives  70.7 us (40%)
  waiting for transfers between devices  39.9 us (22%)
  starting transfers between devices  33.5 us (19%)
  Pallas kernels  22.9 us (13%)
  between operations  4.16 us (2%)
  other arithmetic  3.95 us (2%)
    all_to_all x1, blocking collectives, body(): lax.all_to_all(joined, 'dom', 0, 0, axis_index_groups=same_core, tiled=True)  39.3 us
    all_to_all x1, blocking collectives, body(): lax.all_to_all(partial.reshape(rep_size, rows, width), 'rep', 0, 0, tiled...  31.4 us
    ppermute x9, starting transfers between devices, exchange(): lax.ppermute(value, axis, [(place, place ^ bit) for place in range(size)])  23 us
    all_to_all x1, waiting for transfers between devices, body(): lax.all_to_all(copies_of(node_features, chips), 'dom', 0, 0, axis_index_g...  21.9 us
    ppermute x9, waiting for transfers between devices, exchange(): lax.ppermute(value, axis, [(place, place ^ bit) for place in range(size)])  18 us
    pallas_call x2, Pallas kernels, spread(): pl.pallas_call(functools.partial(spread_kernel, flipped, len(sources)), o...  16.1 us
    all_to_all x1, starting transfers between devices, body(): lax.all_to_all(copies_of(node_features, chips), 'dom', 0, 0, axis_index_g...  6.89 us
    all_to_all x1, starting transfers between devices, body(): lax.all_to_all(grads, 'rep', 0, 0, tiled=True)  3.61 us
  transfers between devices with their start and end apart: 11, of which 8 were waited for; matrix products, arithmetic and copies ran while one was open for 2% of the time, Pallas kernels for 0%

profile of v3, /device:TPU:1, one launch (start us, length us, event | category | flops | bytes accessed | tf_op | source)
XLA Modules:
  0.0 175.1 jit_solution(3049276405062475864)
XLA Ops:
  0.6 2.4 %copies.1 = bf16[8,512,256]{2,1,0:T(8,128)(2,1)} custom-call(bf16[512,256]{1,0:T(8,128)(2,1)} %value_ref.1), custom_call_target="tpu_custom_call" | custom-call | tf_op jit(solution)/shard_map/copies/pallas_call | solution.py:133
  3.0 6.9 %all-to-all-start = ((bf16[8,512,256]{2,1,0:T(8,128)(2,1)}), bf16[8,512,256]{2,1,0:T(8,128)(2,1)S(1)}, u32[]{:S(2)}, u32[]{:S(2)}) async-start(bf16[8,512,256]{2,1,0:T(8,128)(2,1)} %copies.1), calls=%async_computation | async-start | bytes 4194304 | tf_op jit(solution)/shard_map/all_to_all | solution.py:234
  10.7 0.7 select_reduce_fusion.11
  12.2 0.7 select_reduce_fusion.13
  14.2 21.9 %all-to-all-done = bf16[8,512,256]{2,1,0:T(8,128)(2,1)S(1)} async-done(((bf16[8,512,256]{2,1,0:T(8,128)(2,1)}), bf16[8,512,256]{2,1,0:T(8,128)(2,1)S(1)}, u32[]{:S(2)}, u32[]{:S(2)}) %all-to-all-start) | async-done | bytes 2097184 | tf_op jit(solution)/shard_map/all_to_all | solution.py:234
  36.1 0.8 collective-permute-start
  37.4 0.2 convert_reduce_fusion.1
  37.6 0.3 convert_reduce_fusion
  37.9 1.2 select_reduce_fusion
  39.1 1.6 collective-permute-done
  40.7 8.0 %spread_forward.1 = bf16[32,128,256]{2,1,0:T(8,128)(2,1)S(1)} custom-call(s32[2]{0:T(128)S(1)} %pad_add_fusion.turns_ref, s32[640]{0:T(1024)S(1)} %broadcast_add_fusion.1.tile_ref, s32[640]{0:T(1024)S(1)} %get-tuple-element.24.pick_ref, s32[640]{0:T(1024)S(1)} %get-tuple-element.23.place_ref, bf16[512,128,128]{2,1,0:T(8,128)(2,1)} %bitcast.23, ...), custom_call_target="tpu_custom_call" | custom-call | flops 4294967296 | bytes 20971520 | tf_op jit(solution)/shard_map/spread_forward/pallas_call | solution.py:99
  48.7 31.4 %all_to_all.20.parts_ref = bf16[8,512,256]{2,1,0:T(8,128)(2,1)S(1)} all-to-all(bf16[8,512,256]{2,1,0:T(8,128)(2,1)S(1)} %bitcast.18), channel_id=1, replica_groups=mesh['dom'=16,'rep'=8] {'rep'}, dimensions={0} | all-to-all | bytes 4194304 | tf_op jit(solution)/shard_map/all_to_all | solution.py:238
  80.1 2.8 %middle.1 = (bf16[512,256]{1,0:T(8,128)(2,1)}, bf16[8,512,256]{2,1,0:T(8,128)(2,1)}, f32[256,256]{1,0:T(8,128)S(1)}) custom-call(bf16[8,512,256]{2,1,0:T(8,128)(2,1)S(1)} %all_to_all.20.parts_ref, bf16[256,256]{1,0:T(8,128)(2,1)S(1)} %copy-done, bf16[512,256]{1,0:T(8,128)(2,1)S(1)} %copy-done.1), custom_call_target="tpu_custom_call" | custom-call | tf_op jit(solution)/shard_map/middle/pallas_call | solution.py:240
  82.8 3.6 %all-to-all-start.2 = ((bf16[8,512,256]{2,1,0:T(8,128)(2,1)}), bf16[8,512,256]{2,1,0:T(8,128)(2,1)S(1)}, u32[]{:S(2)}, u32[]{:S(2)}) async-start(bf16[8,512,256]{2,1,0:T(8,128)(2,1)} %get-tuple-element.13), calls=%async_computation.2 | async-start | bytes 4194304 | tf_op jit(solution)/shard_map/all_to_all | solution.py:253
  86.5 5.2 %collective-permute-start.1 = (f32[128,256]{1,0:T(8,128)S(1)}, f32[128,256]{1,0:T(8,128)S(1)}, u32[]{:S(2)}, u32[]{:S(2)}) collective-permute-start(f32[128,256]{1,0:T(8,128)S(1)} %slice_select_fusion), channel_id=1, source_target_pairs={{0,16},{8,24},{16,0},{24,8},{32,48},{40,56},{48,32},{56,40},{64,80... | collective-permute-start | bytes 393224 | tf_op jit(solution)/shard_map/ppermute | solution.py:195
  91.6 2.4 %collective-permute-done.1 = f32[128,256]{1,0:T(8,128)S(1)} collective-permute-done((f32[128,256]{1,0:T(8,128)S(1)}, f32[128,256]{1,0:T(8,128)S(1)}, u32[]{:S(2)}, u32[]{:S(2)}) %collective-permute-start.1) | collective-permute-done | bytes 131104 | tf_op jit(solution)/shard_map/ppermute | solution.py:195
  94.0 5.8 %collective-permute-start.2 = (f32[64,256]{1,0:T(8,128)S(1)}, f32[64,256]{1,0:T(8,128)S(1)}, u32[]{:S(2)}, u32[]{:S(2)}) collective-permute-start(f32[64,256]{1,0:T(8,128)S(1)} %slice_select_fusion.1), channel_id=1, source_target_pairs={{0,32},{8,40},{16,48},{24,56},{32,0},{40,8},{48,16},{56,24},{64,96... | collective-permute-start | bytes 196616 | tf_op jit(solution)/shard_map/ppermute | solution.py:195
  99.9 2.0 %collective-permute-done.2 = f32[64,256]{1,0:T(8,128)S(1)} collective-permute-done((f32[64,256]{1,0:T(8,128)S(1)}, f32[64,256]{1,0:T(8,128)S(1)}, u32[]{:S(2)}, u32[]{:S(2)}) %collective-permute-start.2) | collective-permute-done | bytes 65568 | tf_op jit(solution)/shard_map/ppermute | solution.py:195
  101.8 1.8 %collective-permute-start.3 = (f32[64,256]{1,0:T(8,128)S(1)}, f32[64,256]{1,0:T(8,128)S(1)}, u32[]{:S(2)}, u32[]{:S(2)}) collective-permute-start(f32[64,256]{1,0:T(8,128)S(1)} %select_add_fusion.1), channel_id=1, source_target_pairs={{0,8},{8,0},{16,24},{24,16},{32,40},{40,32},{48,56},{56,48},{64,72... | collective-permute-start | bytes 196616 | tf_op jit(solution)/shard_map/ppermute | solution.py:195
  104.3 0.3 collective-permute-done.3
  104.6 3.0 %collective-permute-start.4 = (f32[64,256]{1,0:T(8,128)S(1)}, f32[64,256]{1,0:T(8,128)S(1)}, u32[]{:S(2)}, u32[]{:S(2)}) collective-permute-start(f32[64,256]{1,0:T(8,128)S(1)} %add.269), channel_id=1, source_target_pairs={{0,4},{1,5},{2,6},{3,7},{4,0},{5,1},{6,2},{7,3},{8,12},{9,13},{10,... | collective-permute-start | bytes 196616 | tf_op jit(solution)/shard_map/ppermute | solution.py:195
  107.7 8.5 %collective-permute-done.4 = f32[64,256]{1,0:T(8,128)S(1)} collective-permute-done((f32[64,256]{1,0:T(8,128)S(1)}, f32[64,256]{1,0:T(8,128)S(1)}, u32[]{:S(2)}, u32[]{:S(2)}) %collective-permute-start.4) | collective-permute-done | bytes 65568 | tf_op jit(solution)/shard_map/ppermute | solution.py:195
  116.2 8.2 %spread_back.1 = (f32[32,128,256]{2,1,0:T(8,128)S(1)}, bf16[32,128,256]{2,1,0:T(8,128)(2,1)S(1)}) custom-call(s32[2]{0:T(128)S(1)} %pad_add_fusion.1.turns_ref, s32[640]{0:T(1024)S(1)} %broadcast_add_fusion.tile_ref, s32[640]{0:T(1024)S(1)} %get-tuple-element.22.pick_ref, s32[640]{0:T(1024)S(1)} %get-tuple-element.21.place_ref, ...), custom_call_target="tpu_custom_call" | custom-call | flops 4294967296 | bytes 18874368 | tf_op jit(solution)/shard_map/spread_back/pallas_call | solution.py:99
  124.4 2.5 %collective-permute-start.5 = (bf16[8,512,256]{2,1,0:T(8,128)(2,1)S(1)}, bf16[8,512,256]{2,1,0:T(8,128)(2,1)S(1)}, u32[]{:S(2)}, u32[]{:S(2)}) collective-permute-start(bf16[8,512,256]{2,1,0:T(8,128)(2,1)S(1)} %bitcast.22), channel_id=1, source_target_pairs={{0,8},{8,0},{16,24},{24,16},{32,40},{40,32},{48,56},{56,48},{64,72... | collective-permute-start | bytes 6291464 | tf_op jit(solution)/shard_map/ppermute | solution.py:195
  126.9 1.3 collective-permute-start.8
  128.1 1.4 collective-permute-start.7
  129.5 1.3 collective-permute-start.6
  130.8 1.0 collective-permute-done.8
  131.7 2.4 %collective-permute-done.6 = f32[64,256]{1,0:T(8,128)S(1)} collective-permute-done((f32[64,256]{1,0:T(8,128)S(1)}, f32[64,256]{1,0:T(8,128)S(1)}, u32[]{:S(2)}, u32[]{:S(2)}) %collective-permute-start.6) | collective-permute-done | bytes 65568 | tf_op jit(solution)/shard_map/ppermute | solution.py:195
  134.1 0.5 join.1
  134.7 39.3 %all_to_all.21.parts_ref = bf16[8,576,256]{2,1,0:T(8,128)(2,1)S(1)} all-to-all(bf16[8,576,256]{2,1,0:T(8,128)(2,1)S(1)} %join.1), channel_id=1, replica_groups={{0,16,32,48,64,80,96,112},{8,24,40,56,72,88,104,120},{1,17,33,49,65,81,..., dimensions={0} | all-to-all | bytes 4718592 | tf_op jit(solution)/shard_map/all_to_all | solution.py:282
  174.0 1.1 last.1
  (34 shorter events, 1.0 us)
Async XLA Ops:
  3.0 7.6 %copy-start.3 = (s32[1,1,512]{2,1,0:T(1,128)S(1)}, s32[1,1,512]{2,1,0:T(1,128)}, u32[]{:S(2)}) copy-start(s32[1,1,512]{2,1,0:T(1,128)} %param.11) | copy-start | bytes 6148
  3.0 9.0 %copy-start.2 = (s32[1,1,512]{2,1,0:T(1,128)S(1)}, s32[1,1,512]{2,1,0:T(1,128)}, u32[]{:S(2)}) copy-start(s32[1,1,512]{2,1,0:T(1,128)} %param.10) | copy-start | bytes 6148
  3.0 33.0 %all-to-all-start = ((bf16[8,512,256]{2,1,0:T(8,128)(2,1)}), bf16[8,512,256]{2,1,0:T(8,128)(2,1)S(1)}, u32[]{:S(2)}, u32[]{:S(2)}) async-start(bf16[8,512,256]{2,1,0:T(8,128)(2,1)} %copies.1), calls=%async_computation | async-start | bytes 4194304 | tf_op jit(solution)/shard_map/all_to_all | solution.py:234
  36.1 4.6 %collective-permute-start = (bf16[8,512,256]{2,1,0:T(8,128)(2,1)S(1)}, bf16[8,512,256]{2,1,0:T(8,128)(2,1)S(1)}, u32[]{:S(2)}, u32[]{:S(2)}) collective-permute-start(bf16[8,512,256]{2,1,0:T(8,128)(2,1)S(1)} %all-to-all-done), channel_id=1, source_target_pairs={{0,8},{8,0},{16,24},{24,16},{32,40},{40,32},{48,56},{56,48},{64,72... | collective-permute-start | bytes 6291464 | tf_op jit(solution)/shard_map/ppermute | solution.py:195
  48.7 31.4 %copy-start = (bf16[256,256]{1,0:T(8,128)(2,1)S(1)}, bf16[256,256]{1,0:T(8,128)(2,1)}, u32[]{:S(2)}) copy-start(bf16[256,256]{1,0:T(8,128)(2,1)} %weight_ref.3) | copy-start | bytes 393220
  48.7 31.4 %copy-start.1 = (bf16[512,256]{1,0:T(8,128)(2,1)S(1)}, bf16[512,256]{1,0:T(8,128)(2,1)}, u32[]{:S(2)}) copy-start(bf16[512,256]{1,0:T(8,128)(2,1)} %cotangent_ref.1) | copy-start | bytes 786436
  82.8 33.4 %all-to-all-start.2 = ((bf16[8,512,256]{2,1,0:T(8,128)(2,1)}), bf16[8,512,256]{2,1,0:T(8,128)(2,1)S(1)}, u32[]{:S(2)}, u32[]{:S(2)}) async-start(bf16[8,512,256]{2,1,0:T(8,128)(2,1)} %get-tuple-element.13), calls=%async_computation.2 | async-start | bytes 4194304 | tf_op jit(solution)/shard_map/all_to_all | solution.py:253
  86.5 7.5 %collective-permute-start.1 = (f32[128,256]{1,0:T(8,128)S(1)}, f32[128,256]{1,0:T(8,128)S(1)}, u32[]{:S(2)}, u32[]{:S(2)}) collective-permute-start(f32[128,256]{1,0:T(8,128)S(1)} %slice_select_fusion), channel_id=1, source_target_pairs={{0,16},{8,24},{16,0},{24,8},{32,48},{40,56},{48,32},{56,40},{64,80... | collective-permute-start | bytes 393224 | tf_op jit(solution)/shard_map/ppermute | solution.py:195
  94.0 7.8 %collective-permute-start.2 = (f32[64,256]{1,0:T(8,128)S(1)}, f32[64,256]{1,0:T(8,128)S(1)}, u32[]{:S(2)}, u32[]{:S(2)}) collective-permute-start(f32[64,256]{1,0:T(8,128)S(1)} %slice_select_fusion.1), channel_id=1, source_target_pairs={{0,32},{8,40},{16,48},{24,56},{32,0},{40,8},{48,16},{56,24},{64,96... | collective-permute-start | bytes 196616 | tf_op jit(solution)/shard_map/ppermute | solution.py:195
  101.8 2.7 %collective-permute-start.3 = (f32[64,256]{1,0:T(8,128)S(1)}, f32[64,256]{1,0:T(8,128)S(1)}, u32[]{:S(2)}, u32[]{:S(2)}) collective-permute-start(f32[64,256]{1,0:T(8,128)S(1)} %select_add_fusion.1), channel_id=1, source_target_pairs={{0,8},{8,0},{16,24},{24,16},{32,40},{40,32},{48,56},{56,48},{64,72... | collective-permute-start | bytes 196616 | tf_op jit(solution)/shard_map/ppermute | solution.py:195
  104.6 11.6 %collective-permute-start.4 = (f32[64,256]{1,0:T(8,128)S(1)}, f32[64,256]{1,0:T(8,128)S(1)}, u32[]{:S(2)}, u32[]{:S(2)}) collective-permute-start(f32[64,256]{1,0:T(8,128)S(1)} %add.269), channel_id=1, source_target_pairs={{0,4},{1,5},{2,6},{3,7},{4,0},{5,1},{6,2},{7,3},{8,12},{9,13},{10,... | collective-permute-start | bytes 196616 | tf_op jit(solution)/shard_map/ppermute | solution.py:195
  124.4 9.7 %collective-permute-start.5 = (bf16[8,512,256]{2,1,0:T(8,128)(2,1)S(1)}, bf16[8,512,256]{2,1,0:T(8,128)(2,1)S(1)}, u32[]{:S(2)}, u32[]{:S(2)}) collective-permute-start(bf16[8,512,256]{2,1,0:T(8,128)(2,1)S(1)} %bitcast.22), channel_id=1, source_target_pairs={{0,8},{8,0},{16,24},{24,16},{32,40},{40,32},{48,56},{56,48},{64,72... | collective-permute-start | bytes 6291464 | tf_op jit(solution)/shard_map/ppermute | solution.py:195
  126.9 4.9 %collective-permute-start.8 = (f32[64,256]{1,0:T(8,128)S(1)}, f32[64,256]{1,0:T(8,128)S(1)}, u32[]{:S(2)}, u32[]{:S(2)}) collective-permute-start(f32[64,256]{1,0:T(8,128)S(1)} %add.270), channel_id=1, source_target_pairs={{0,3},{1,2},{2,1},{3,0},{4,7},{5,6},{6,5},{7,4},{8,11},{9,10},{10,... | collective-permute-start | bytes 196616 | tf_op jit(solution)/shard_map/ppermute | solution.py:195
  128.1 3.6 %collective-permute-start.7 = (f32[64,256]{1,0:T(8,128)S(1)}, f32[64,256]{1,0:T(8,128)S(1)}, u32[]{:S(2)}, u32[]{:S(2)}) collective-permute-start(f32[64,256]{1,0:T(8,128)S(1)} %add.270), channel_id=1, source_target_pairs={{0,1},{1,0},{2,3},{3,2},{4,5},{5,4},{6,7},{7,6},{8,9},{9,8},{10,11... | collective-permute-start | bytes 196616 | tf_op jit(solution)/shard_map/ppermute | solution.py:195
  129.5 4.6 %collective-permute-start.6 = (f32[64,256]{1,0:T(8,128)S(1)}, f32[64,256]{1,0:T(8,128)S(1)}, u32[]{:S(2)}, u32[]{:S(2)}) collective-permute-start(f32[64,256]{1,0:T(8,128)S(1)} %add.270), channel_id=1, source_target_pairs={{0,2},{1,3},{2,0},{3,1},{4,6},{5,7},{6,4},{7,5},{8,10},{9,11},{10,... | collective-permute-start | bytes 196616 | tf_op jit(solution)/shard_map/ppermute | solution.py:195

commit v4 on v3

--- a/solution.py
+++ b/solution.py
@@ -1,4 +1,5 @@
 import functools
+import math
 
 import jax
 import jax.numpy as jnp
@@ -165,33 +166,31 @@
         copy.wait()
 
 
-def join_kernel(own_ref, other_ref, term_ref, send_ref):
-    rows = own_ref.shape[1]
-    send_ref[0, :rows, :] = (own_ref[0] + other_ref[0].astype(jnp.float32)).astype(jnp.bfloat16)
-    send_ref[0, rows:, :] = term_ref[...].astype(jnp.bfloat16)
-
-
-def last_kernel(parts_ref, weight_ref, out_ref, term_ref):
-    members = parts_ref.shape[0]
-    rows = out_ref.shape[0]
-    share = parts_ref.shape[1] - rows
-    pieces = term_ref.shape[0] // share
-    grad = parts_ref[0, :rows].astype(jnp.float32)
-    for member in range(1, members):
-        grad += parts_ref[member, :rows].astype(jnp.float32)
+def join_kernel(own_ref, other_ref, send_ref, sum_ref, sems):
+    copies = [pltpu.make_async_copy(sum_ref.at[i], send_ref.at[i], sems.at[i]) for i in range(sum_ref.shape[0])]
+    for i, copy in enumerate(copies):
+        sum_ref[i] = (own_ref[i] + other_ref[i].astype(jnp.float32)).astype(jnp.bfloat16)
+        copy.start()
+    for copy in copies:
+        copy.wait()
+
+
+def last_kernel(parts_ref, weight_ref, out_ref):
+    grad = parts_ref[0].astype(jnp.float32)
+    for member in range(1, parts_ref.shape[0]):
+        grad += parts_ref[member].astype(jnp.float32)
     out_ref[...] = lax.dot_general(
         grad.astype(jnp.bfloat16), weight_ref[...], (((1,), (1,)), ((), ())), preferred_element_type=jnp.float32
     ).astype(out_ref.dtype)
-    for piece in range(pieces):
-        place = sum(((piece >> bit) & 1) * (term_ref.shape[0] >> (bit + 1)) for bit in range(pieces.bit_length() - 1))
-        total = parts_ref[piece, rows:].astype(jnp.float32)
-        for member in range(piece + pieces, members, pieces):
-            total += parts_ref[member, rows:].astype(jnp.float32)
-        term_ref[place : place + share, :] = total
+
+
+def ordered(value, other, axis, bit):
+    upper = (lax.axis_index(axis) & bit) != 0
+    return jnp.concatenate([jnp.where(upper, other, value), jnp.where(upper, value, other)], axis=0)
 
 
 def exchange(value, axis, bit):
-    size = lax.axis_size(axis)
+    size = math.prod(lax.axis_size(name) for name in ((axis,) if isinstance(axis, str) else axis))
     return lax.ppermute(value, axis, [(place, place ^ bit) for place in range(size)])
 
 
@@ -210,7 +209,6 @@
     own = rows // BLOCK
     chips = dom_size // 2
     pieces = chips // 2
-    wide = rows + width // pieces
     params = pltpu.CompilerParams(vmem_limit_bytes=24 << 20)
     row_index = tile_row.reshape(slots)
     col_index = tile_col.reshape(slots)
@@ -257,7 +255,9 @@
         term = halve(term, "dom", bit)
         bit *= 2
     term = term + exchange(term, "dom", 1)
-    term = term + exchange(term, "rep", rep_size // 2)
+    across = [("dom", "rep"), ("dom", dom_size // 2), ("rep", rep_size // 2)]
+    both = exchange(term, across[0], (dom_size // 2) * rep_size + rep_size // 2)
+    term = (term + exchange(term, *across[1])) + (exchange(term, *across[2]) + both)
     grads, term = lax.optimization_barrier((grads, term))
 
     mine, other = spread(
@@ -265,27 +265,25 @@
     )
     mine, other = mine.reshape(chips, rows, width), other.reshape(chips, rows, width)
     other = exchange(other, "dom", 1)
-    term = (term + exchange(term, "rep", 2)) + (exchange(term, "rep", 1) + exchange(term, "rep", 3))
     joined = pl.pallas_call(
         join_kernel,
-        grid=(chips,),
-        out_shape=jax.ShapeDtypeStruct((chips, wide, width), jnp.bfloat16),
-        in_specs=[
-            pl.BlockSpec((1, rows, width), lambda i: (i, 0, 0)),
-            pl.BlockSpec((1, rows, width), lambda i: (i, 0, 0)),
-            pl.BlockSpec((width // pieces, width), lambda i: (0, 0)),
-        ],
-        out_specs=pl.BlockSpec((1, wide, width), lambda i: (i, 0, 0)),
+        out_shape=pltpu.HBM((chips, rows, width), jnp.bfloat16),
+        in_specs=[in_vmem] * 2,
+        out_specs=pl.BlockSpec(memory_space=pltpu.HBM),
+        scratch_shapes=[pltpu.VMEM((chips, rows, width), jnp.bfloat16), pltpu.SemaphoreType.DMA((chips,))],
         compiler_params=params,
         name="join",
-    )(mine, other, term)
+    )(mine, other)
+    joined, term = lax.optimization_barrier((joined, term))
     back_parts = lax.all_to_all(joined, "dom", 0, 0, axis_index_groups=same_core, tiled=True)
-    grad_features, grad_weight = pl.pallas_call(
+    term = (term + exchange(term, "rep", 2)) + (exchange(term, "rep", 1) + exchange(term, "rep", 3))
+    near_half = ordered(term, exchange(term, "dom", 4), "dom", 4)
+    far_half = ordered(exchange(term, "dom", 2), exchange(term, "dom", 6), "dom", 4)
+    grad_weight = ordered(near_half, far_half, "dom", 2)
+    back_parts, grad_weight = lax.optimization_barrier((back_parts, grad_weight))
+    grad_features = pl.pallas_call(
         last_kernel,
-        out_shape=(
-            jax.ShapeDtypeStruct((rows, width), jnp.bfloat16),
-            jax.ShapeDtypeStruct((width, width), jnp.float32),
-        ),
+        out_shape=jax.ShapeDtypeStruct((rows, width), jnp.bfloat16),
         compiler_params=params,
         name="last",
     )(back_parts, weight)

time: 178 us -> 175 us (0.983); the launches traced: 175 us -> 176 us
  blocking collectives: 70.7 us -> 36 us
  waiting for transfers between devices: 39.9 us -> 63.3 us
  starting transfers between devices: 33.5 us -> 41.4 us
  Pallas kernels: 22.9 us -> 25.8 us
    all_to_all x1 -> x0, blocking collectives: 39.3 us -> none  [body(): lax.all_to_all(joined, 'dom', 0, 0, axis_index_groups=same_core, tiled=True)]
    ppermute x9 -> x14, waiting for transfers between devices: 18 us -> 41.5 us  [exchange(): lax.ppermute(value, axis, [(place, place ^ bit) for place in range(size)])]
    all_to_all x0 -> x1, starting transfers between devices: none -> 6.5 us  [body(): lax.all_to_all(joined, 'dom', 0, 0, axis_index_groups=same_core, tiled=True)]
    all_to_all x1, blocking collectives: 31.4 us -> 36 us  [body(): lax.all_to_all(partial.reshape(rep_size, rows, width), 'rep', 0, 0, tiled...]
    pallas_call x2, Pallas kernels: 16.1 us -> 18.1 us  [spread(): pl.pallas_call(functools.partial(spread_kernel, flipped, len(sources)), o...]
    ppermute x9 -> x14, starting transfers between devices: 23 us -> 24.4 us  [exchange(): lax.ppermute(value, axis, [(place, place ^ bit) for place in range(size)])]
  transfers between devices with their start and end apart: 11 -> 17, of which waited for: 8 -> 13; matrix products, arithmetic and copies ran while one was open for 2% -> 3% of each run, Pallas kernels for 0% -> 0%
where the time goes in v4:
time: 175 us; the launch traced here: 176 us
  waiting for transfers between devices  63.3 us (36%)
  starting transfers between devices  41.4 us (24%)
  blocking collectives  36 us (21%)
  Pallas kernels  25.8 us (15%)
  other arithmetic  4.73 us (3%)
  between operations  4.17 us (2%)
    ppermute x14, waiting for transfers between devices, exchange(): lax.ppermute(value, axis, [(place, place ^ bit) for place in range(size)])  41.5 us
    all_to_all x1, blocking collectives, body(): lax.all_to_all(partial.reshape(rep_size, rows, width), 'rep', 0, 0, tiled...  36 us
    ppermute x14, starting transfers between devices, exchange(): lax.ppermute(value, axis, [(place, place ^ bit) for place in range(size)])  24.4 us
    all_to_all x1, waiting for transfers between devices, body(): lax.all_to_all(copies_of(node_features, chips), 'dom', 0, 0, axis_index_g...  21.9 us
    pallas_call x2, Pallas kernels, spread(): pl.pallas_call(functools.partial(spread_kernel, flipped, len(sources)), o...  18.1 us
    all_to_all x1, starting transfers between devices, body(): lax.all_to_all(copies_of(node_features, chips), 'dom', 0, 0, axis_index_g...  6.89 us
    all_to_all x1, starting transfers between devices, body(): lax.all_to_all(joined, 'dom', 0, 0, axis_index_groups=same_core, tiled=True)  6.5 us
    all_to_all x1, starting transfers between devices, body(): lax.all_to_all(grads, 'rep', 0, 0, tiled=True)  3.61 us
  transfers between devices with their start and end apart: 17, of which 13 were waited for; matrix products, arithmetic and copies ran while one was open for 3% of the time, Pallas kernels for 0%

profile of v4, /device:TPU:1, one launch (start us, length us, event | category | flops | bytes accessed | tf_op | source)
XLA Modules:
  0.0 175.5 jit_solution(11228711055099421213)
XLA Ops:
  0.6 2.4 %copies.1 = bf16[8,512,256]{2,1,0:T(8,128)(2,1)} custom-call(bf16[512,256]{1,0:T(8,128)(2,1)} %value_ref.1), custom_call_target="tpu_custom_call" | custom-call | tf_op jit(solution)/shard_map/copies/pallas_call | solution.py:134
  3.0 6.9 %all-to-all-start = ((bf16[8,512,256]{2,1,0:T(8,128)(2,1)}), bf16[8,512,256]{2,1,0:T(8,128)(2,1)S(1)}, u32[]{:S(2)}, u32[]{:S(2)}) async-start(bf16[8,512,256]{2,1,0:T(8,128)(2,1)} %copies.1), calls=%async_computation | async-start | bytes 4194304 | tf_op jit(solution)/shard_map/all_to_all | solution.py:232
  14.2 21.9 %all-to-all-done = bf16[8,512,256]{2,1,0:T(8,128)(2,1)S(1)} async-done(((bf16[8,512,256]{2,1,0:T(8,128)(2,1)}), bf16[8,512,256]{2,1,0:T(8,128)(2,1)S(1)}, u32[]{:S(2)}, u32[]{:S(2)}) %all-to-all-start) | async-done | bytes 2097184 | tf_op jit(solution)/shard_map/all_to_all | solution.py:232
  36.1 0.8 collective-permute-start
  37.9 1.2 select_reduce_fusion
  39.1 1.6 collective-permute-done
  40.7 9.0 %spread_forward.1 = bf16[32,128,256]{2,1,0:T(8,128)(2,1)S(1)} custom-call(s32[2]{0:T(128)S(1)} %pad_add_fusion.turns_ref, s32[640]{0:T(1024)S(1)} %broadcast_add_fusion.1.tile_ref, s32[640]{0:T(1024)S(1)} %get-tuple-element.28.pick_ref, s32[640]{0:T(1024)S(1)} %get-tuple-element.27.place_ref, bf16[512,128,128]{2,1,0:T(8,128)(2,1)} %bitcast.23, ...), custom_call_target="tpu_custom_call" | custom-call | flops 4294967296 | bytes 20971520 | tf_op jit(solution)/shard_map/spread_forward/pallas_call | solution.py:100
  49.7 36.0 %all_to_all.20.parts_ref = bf16[8,512,256]{2,1,0:T(8,128)(2,1)S(1)} all-to-all(bf16[8,512,256]{2,1,0:T(8,128)(2,1)S(1)} %bitcast.18), channel_id=1, replica_groups=mesh['dom'=16,'rep'=8] {'rep'}, dimensions={0} | all-to-all | bytes 4194304 | tf_op jit(solution)/shard_map/all_to_all | solution.py:236
  85.7 2.8 %middle.1 = (bf16[512,256]{1,0:T(8,128)(2,1)}, bf16[8,512,256]{2,1,0:T(8,128)(2,1)}, f32[256,256]{1,0:T(8,128)S(1)}) custom-call(bf16[8,512,256]{2,1,0:T(8,128)(2,1)S(1)} %all_to_all.20.parts_ref, bf16[256,256]{1,0:T(8,128)(2,1)S(1)} %copy-done, bf16[512,256]{1,0:T(8,128)(2,1)S(1)} %copy-done.1), custom_call_target="tpu_custom_call" | custom-call | tf_op jit(solution)/shard_map/middle/pallas_call | solution.py:238
  88.5 3.6 %all-to-all-start.2 = ((bf16[8,512,256]{2,1,0:T(8,128)(2,1)}), bf16[8,512,256]{2,1,0:T(8,128)(2,1)S(1)}, u32[]{:S(2)}, u32[]{:S(2)}) async-start(bf16[8,512,256]{2,1,0:T(8,128)(2,1)} %get-tuple-element.15), calls=%async_computation.2 | async-start | bytes 4194304 | tf_op jit(solution)/shard_map/all_to_all | solution.py:251
  92.1 1.9 %collective-permute-start.1 = (f32[128,256]{1,0:T(8,128)S(1)}, f32[128,256]{1,0:T(8,128)S(1)}, u32[]{:S(2)}, u32[]{:S(2)}) collective-permute-start(f32[128,256]{1,0:T(8,128)S(1)} %slice_select_fusion), channel_id=1, source_target_pairs={{0,16},{8,24},{16,0},{24,8},{32,48},{40,56},{48,32},{56,40},{64,80... | collective-permute-start | bytes 393224 | tf_op jit(solution)/shard_map/ppermute | solution.py:194
  94.0 2.4 %collective-permute-done.1 = f32[128,256]{1,0:T(8,128)S(1)} collective-permute-done((f32[128,256]{1,0:T(8,128)S(1)}, f32[128,256]{1,0:T(8,128)S(1)}, u32[]{:S(2)}, u32[]{:S(2)}) %collective-permute-start.1) | collective-permute-done | bytes 131104 | tf_op jit(solution)/shard_map/ppermute | solution.py:194
  96.5 3.2 %collective-permute-start.2 = (f32[64,256]{1,0:T(8,128)S(1)}, f32[64,256]{1,0:T(8,128)S(1)}, u32[]{:S(2)}, u32[]{:S(2)}) collective-permute-start(f32[64,256]{1,0:T(8,128)S(1)} %slice_select_fusion.1), channel_id=1, source_target_pairs={{0,32},{8,40},{16,48},{24,56},{32,0},{40,8},{48,16},{56,24},{64,96... | collective-permute-start | bytes 196616 | tf_op jit(solution)/shard_map/ppermute | solution.py:194
  99.7 2.0 %collective-permute-done.2 = f32[64,256]{1,0:T(8,128)S(1)} collective-permute-done((f32[64,256]{1,0:T(8,128)S(1)}, f32[64,256]{1,0:T(8,128)S(1)}, u32[]{:S(2)}, u32[]{:S(2)}) %collective-permute-start.2) | collective-permute-done | bytes 65568 | tf_op jit(solution)/shard_map/ppermute | solution.py:194
  101.7 3.8 %collective-permute-start.3 = (f32[64,256]{1,0:T(8,128)S(1)}, f32[64,256]{1,0:T(8,128)S(1)}, u32[]{:S(2)}, u32[]{:S(2)}) collective-permute-start(f32[64,256]{1,0:T(8,128)S(1)} %select_add_fusion.1), channel_id=1, source_target_pairs={{0,8},{8,0},{16,24},{24,16},{32,40},{40,32},{48,56},{56,48},{64,72... | collective-permute-start | bytes 196616 | tf_op jit(solution)/shard_map/ppermute | solution.py:194
  106.4 1.9 %collective-permute-start.6 = (f32[64,256]{1,0:T(8,128)S(1)}, f32[64,256]{1,0:T(8,128)S(1)}, u32[]{:S(2)}, u32[]{:S(2)}) collective-permute-start(f32[64,256]{1,0:T(8,128)S(1)} %add.275), channel_id=1, source_target_pairs={{0,68},{1,69},{2,70},{3,71},{4,64},{5,65},{6,66},{7,67},{8,76},{9,... | collective-permute-start | bytes 196616 | tf_op jit(solution)/shard_map/ppermute | solution.py:194
  108.3 1.4 collective-permute-start.5
  109.8 11.8 %collective-permute-done.6 = f32[64,256]{1,0:T(8,128)S(1)} collective-permute-done((f32[64,256]{1,0:T(8,128)S(1)}, f32[64,256]{1,0:T(8,128)S(1)}, u32[]{:S(2)}, u32[]{:S(2)}) %collective-permute-start.6) | collective-permute-done | bytes 65568 | tf_op jit(solution)/shard_map/ppermute | solution.py:194
  121.7 9.2 %spread_back.1 = (f32[32,128,256]{2,1,0:T(8,128)S(1)}, bf16[32,128,256]{2,1,0:T(8,128)(2,1)S(1)}) custom-call(s32[2]{0:T(128)S(1)} %pad_add_fusion.1.turns_ref, s32[640]{0:T(1024)S(1)} %broadcast_add_fusion.tile_ref, s32[640]{0:T(1024)S(1)} %get-tuple-element.26.pick_ref, s32[640]{0:T(1024)S(1)} %get-tuple-element.25.place_ref, ...), custom_call_target="tpu_custom_call" | custom-call | flops 4294967296 | bytes 18874368 | tf_op jit(solution)/shard_map/spread_back/pallas_call | solution.py:100
  130.8 2.5 %collective-permute-start.7 = (bf16[8,512,256]{2,1,0:T(8,128)(2,1)S(1)}, bf16[8,512,256]{2,1,0:T(8,128)(2,1)S(1)}, u32[]{:S(2)}, u32[]{:S(2)}) collective-permute-start(bf16[8,512,256]{2,1,0:T(8,128)(2,1)S(1)} %bitcast.22), channel_id=1, source_target_pairs={{0,8},{8,0},{16,24},{24,16},{32,40},{40,32},{48,56},{56,48},{64,72... | collective-permute-start | bytes 6291464 | tf_op jit(solution)/shard_map/ppermute | solution.py:194
  133.3 3.8 %collective-permute-done.7.other_ref = bf16[8,512,256]{2,1,0:T(8,128)(2,1)S(1)} collective-permute-done((bf16[8,512,256]{2,1,0:T(8,128)(2,1)S(1)}, bf16[8,512,256]{2,1,0:T(8,128)(2,1)S(1)}, u32[]{:S(2)}, u32[]{:S(2)}) %collective-permute-start.7) | collective-permute-done | bytes 2097184 | tf_op jit(solution)/shard_map/ppermute | solution.py:194
  137.1 1.5 join.1
  138.6 6.5 %all-to-all-start.3 = ((bf16[8,512,256]{2,1,0:T(8,128)(2,1)}), bf16[8,512,256]{2,1,0:T(8,128)(2,1)S(1)}, u32[]{:S(2)}, u32[]{:S(2)}) async-start(bf16[8,512,256]{2,1,0:T(8,128)(2,1)} %join.1), calls=%async_computation.3 | async-start | bytes 4194304 | tf_op jit(solution)/shard_map/all_to_all | solution.py:278
  145.1 1.5 collective-permute-start.10
  146.6 2.4 %collective-permute-start.8 = (f32[64,256]{1,0:T(8,128)S(1)}, f32[64,256]{1,0:T(8,128)S(1)}, u32[]{:S(2)}, u32[]{:S(2)}) collective-permute-start(f32[64,256]{1,0:T(8,128)S(1)} %add_add_fusion.1), channel_id=1, source_target_pairs={{0,2},{1,3},{2,0},{3,1},{4,6},{5,7},{6,4},{7,5},{8,10},{9,11},{10,... | collective-permute-start | bytes 196616 | tf_op jit(solution)/shard_map/ppermute | solution.py:194
  149.7 1.9 %collective-permute-done.8 = f32[64,256]{1,0:T(8,128)S(1)} collective-permute-done((f32[64,256]{1,0:T(8,128)S(1)}, f32[64,256]{1,0:T(8,128)S(1)}, u32[]{:S(2)}, u32[]{:S(2)}) %collective-permute-start.8) | collective-permute-done | bytes 65568 | tf_op jit(solution)/shard_map/ppermute | solution.py:194
  151.6 2.9 %collective-permute-start.13 = (f32[64,256]{1,0:T(8,128)S(1)}, f32[64,256]{1,0:T(8,128)S(1)}, u32[]{:S(2)}, u32[]{:S(2)}) collective-permute-start(f32[64,256]{1,0:T(8,128)S(1)} %add_add_fusion), channel_id=1, source_target_pairs={{0,32},{8,40},{16,48},{24,56},{32,0},{40,8},{48,16},{56,24},{64,96... | collective-permute-start | bytes 196616 | tf_op jit(solution)/shard_map/ppermute | solution.py:194
  154.9 1.6 collective-permute-start.11
  156.6 15.5 %collective-permute-done.13 = f32[64,256]{1,0:T(8,128)S(1)} collective-permute-done((f32[64,256]{1,0:T(8,128)S(1)}, f32[64,256]{1,0:T(8,128)S(1)}, u32[]{:S(2)}, u32[]{:S(2)}) %collective-permute-start.13) | collective-permute-done | bytes 65568 | tf_op jit(solution)/shard_map/ppermute | solution.py:194
  172.3 1.4 collective-permute-done.11
  173.7 0.7 pad_maximum_fusion
  174.4 1.1 last.1
  (49 shorter events, 4.6 us)
Async XLA Ops:
  3.0 7.6 %copy-start.3 = (s32[1,1,512]{2,1,0:T(1,128)S(1)}, s32[1,1,512]{2,1,0:T(1,128)}, u32[]{:S(2)}) copy-start(s32[1,1,512]{2,1,0:T(1,128)} %param.11) | copy-start | bytes 6148
  3.0 9.0 %copy-start.2 = (s32[1,1,512]{2,1,0:T(1,128)S(1)}, s32[1,1,512]{2,1,0:T(1,128)}, u32[]{:S(2)}) copy-start(s32[1,1,512]{2,1,0:T(1,128)} %param.10) | copy-start | bytes 6148
  3.0 33.0 %all-to-all-start = ((bf16[8,512,256]{2,1,0:T(8,128)(2,1)}), bf16[8,512,256]{2,1,0:T(8,128)(2,1)S(1)}, u32[]{:S(2)}, u32[]{:S(2)}) async-start(bf16[8,512,256]{2,1,0:T(8,128)(2,1)} %copies.1), calls=%async_computation | async-start | bytes 4194304 | tf_op jit(solution)/shard_map/all_to_all | solution.py:232
  36.1 4.6 %collective-permute-start = (bf16[8,512,256]{2,1,0:T(8,128)(2,1)S(1)}, bf16[8,512,256]{2,1,0:T(8,128)(2,1)S(1)}, u32[]{:S(2)}, u32[]{:S(2)}) collective-permute-start(bf16[8,512,256]{2,1,0:T(8,128)(2,1)S(1)} %all-to-all-done), channel_id=1, source_target_pairs={{0,8},{8,0},{16,24},{24,16},{32,40},{40,32},{48,56},{56,48},{64,72... | collective-permute-start | bytes 6291464 | tf_op jit(solution)/shard_map/ppermute | solution.py:194
  49.7 36.0 %copy-start = (bf16[256,256]{1,0:T(8,128)(2,1)S(1)}, bf16[256,256]{1,0:T(8,128)(2,1)}, u32[]{:S(2)}) copy-start(bf16[256,256]{1,0:T(8,128)(2,1)} %weight_ref.3) | copy-start | bytes 393220
  49.7 36.0 %copy-start.1 = (bf16[512,256]{1,0:T(8,128)(2,1)S(1)}, bf16[512,256]{1,0:T(8,128)(2,1)}, u32[]{:S(2)}) copy-start(bf16[512,256]{1,0:T(8,128)(2,1)} %cotangent_ref.1) | copy-start | bytes 786436
  88.5 33.2 %all-to-all-start.2 = ((bf16[8,512,256]{2,1,0:T(8,128)(2,1)}), bf16[8,512,256]{2,1,0:T(8,128)(2,1)S(1)}, u32[]{:S(2)}, u32[]{:S(2)}) async-start(bf16[8,512,256]{2,1,0:T(8,128)(2,1)} %get-tuple-element.15), calls=%async_computation.2 | async-start | bytes 4194304 | tf_op jit(solution)/shard_map/all_to_all | solution.py:251
  92.1 4.3 %collective-permute-start.1 = (f32[128,256]{1,0:T(8,128)S(1)}, f32[128,256]{1,0:T(8,128)S(1)}, u32[]{:S(2)}, u32[]{:S(2)}) collective-permute-start(f32[128,256]{1,0:T(8,128)S(1)} %slice_select_fusion), channel_id=1, source_target_pairs={{0,16},{8,24},{16,0},{24,8},{32,48},{40,56},{48,32},{56,40},{64,80... | collective-permute-start | bytes 393224 | tf_op jit(solution)/shard_map/ppermute | solution.py:194
  96.5 5.2 %collective-permute-start.2 = (f32[64,256]{1,0:T(8,128)S(1)}, f32[64,256]{1,0:T(8,128)S(1)}, u32[]{:S(2)}, u32[]{:S(2)}) collective-permute-start(f32[64,256]{1,0:T(8,128)S(1)} %slice_select_fusion.1), channel_id=1, source_target_pairs={{0,32},{8,40},{16,48},{24,56},{32,0},{40,8},{48,16},{56,24},{64,96... | collective-permute-start | bytes 196616 | tf_op jit(solution)/shard_map/ppermute | solution.py:194
  101.7 4.7 %collective-permute-start.3 = (f32[64,256]{1,0:T(8,128)S(1)}, f32[64,256]{1,0:T(8,128)S(1)}, u32[]{:S(2)}, u32[]{:S(2)}) collective-permute-start(f32[64,256]{1,0:T(8,128)S(1)} %select_add_fusion.1), channel_id=1, source_target_pairs={{0,8},{8,0},{16,24},{24,16},{32,40},{40,32},{48,56},{56,48},{64,72... | collective-permute-start | bytes 196616 | tf_op jit(solution)/shard_map/ppermute | solution.py:194
  106.4 15.2 %collective-permute-start.6 = (f32[64,256]{1,0:T(8,128)S(1)}, f32[64,256]{1,0:T(8,128)S(1)}, u32[]{:S(2)}, u32[]{:S(2)}) collective-permute-start(f32[64,256]{1,0:T(8,128)S(1)} %add.275), channel_id=1, source_target_pairs={{0,68},{1,69},{2,70},{3,71},{4,64},{5,65},{6,66},{7,67},{8,76},{9,... | collective-permute-start | bytes 196616 | tf_op jit(solution)/shard_map/ppermute | solution.py:194
  108.3 13.3 %collective-permute-start.5 = (f32[64,256]{1,0:T(8,128)S(1)}, f32[64,256]{1,0:T(8,128)S(1)}, u32[]{:S(2)}, u32[]{:S(2)}) collective-permute-start(f32[64,256]{1,0:T(8,128)S(1)} %add.275), channel_id=1, source_target_pairs={{0,4},{1,5},{2,6},{3,7},{4,0},{5,1},{6,2},{7,3},{8,12},{9,13},{10,... | collective-permute-start | bytes 196616 | tf_op jit(solution)/shard_map/ppermute | solution.py:194
  109.7 11.9 %collective-permute-start.4 = (f32[64,256]{1,0:T(8,128)S(1)}, f32[64,256]{1,0:T(8,128)S(1)}, u32[]{:S(2)}, u32[]{:S(2)}) collective-permute-start(f32[64,256]{1,0:T(8,128)S(1)} %add.275), channel_id=1, source_target_pairs={{0,64},{8,72},{16,80},{24,88},{32,96},{40,104},{48,112},{56,120},{... | collective-permute-start | bytes 196616 | tf_op jit(solution)/shard_map/ppermute | solution.py:194
  130.8 6.2 %collective-permute-start.7 = (bf16[8,512,256]{2,1,0:T(8,128)(2,1)S(1)}, bf16[8,512,256]{2,1,0:T(8,128)(2,1)S(1)}, u32[]{:S(2)}, u32[]{:S(2)}) collective-permute-start(bf16[8,512,256]{2,1,0:T(8,128)(2,1)S(1)} %bitcast.22), channel_id=1, source_target_pairs={{0,8},{8,0},{16,24},{24,16},{32,40},{40,32},{48,56},{56,48},{64,72... | collective-permute-start | bytes 6291464 | tf_op jit(solution)/shard_map/ppermute | solution.py:194
  138.6 35.8 %all-to-all-start.3 = ((bf16[8,512,256]{2,1,0:T(8,128)(2,1)}), bf16[8,512,256]{2,1,0:T(8,128)(2,1)S(1)}, u32[]{:S(2)}, u32[]{:S(2)}) async-start(bf16[8,512,256]{2,1,0:T(8,128)(2,1)} %join.1), calls=%async_computation.3 | async-start | bytes 4194304 | tf_op jit(solution)/shard_map/all_to_all | solution.py:278
  145.1 4.3 %collective-permute-start.10 = (f32[64,256]{1,0:T(8,128)S(1)}, f32[64,256]{1,0:T(8,128)S(1)}, u32[]{:S(2)}, u32[]{:S(2)}) collective-permute-start(f32[64,256]{1,0:T(8,128)S(1)} %add_add_fusion.1), channel_id=1, source_target_pairs={{0,3},{1,2},{2,1},{3,0},{4,7},{5,6},{6,5},{7,4},{8,11},{9,10},{10,... | collective-permute-start | bytes 196616 | tf_op jit(solution)/shard_map/ppermute | solution.py:194
  146.5 3.1 %collective-permute-start.9 = (f32[64,256]{1,0:T(8,128)S(1)}, f32[64,256]{1,0:T(8,128)S(1)}, u32[]{:S(2)}, u32[]{:S(2)}) collective-permute-start(f32[64,256]{1,0:T(8,128)S(1)} %add_add_fusion.1), channel_id=1, source_target_pairs={{0,1},{1,0},{2,3},{3,2},{4,5},{5,4},{6,7},{7,6},{8,9},{9,8},{10,11... | collective-permute-start | bytes 196616 | tf_op jit(solution)/shard_map/ppermute | solution.py:194
  146.6 5.0 %collective-permute-start.8 = (f32[64,256]{1,0:T(8,128)S(1)}, f32[64,256]{1,0:T(8,128)S(1)}, u32[]{:S(2)}, u32[]{:S(2)}) collective-permute-start(f32[64,256]{1,0:T(8,128)S(1)} %add_add_fusion.1), channel_id=1, source_target_pairs={{0,2},{1,3},{2,0},{3,1},{4,6},{5,7},{6,4},{7,5},{8,10},{9,11},{10,... | collective-permute-start | bytes 196616 | tf_op jit(solution)/shard_map/ppermute | solution.py:194
  151.6 20.4 %collective-permute-start.13 = (f32[64,256]{1,0:T(8,128)S(1)}, f32[64,256]{1,0:T(8,128)S(1)}, u32[]{:S(2)}, u32[]{:S(2)}) collective-permute-start(f32[64,256]{1,0:T(8,128)S(1)} %add_add_fusion), channel_id=1, source_target_pairs={{0,32},{8,40},{16,48},{24,56},{32,0},{40,8},{48,16},{56,24},{64,96... | collective-permute-start | bytes 196616 | tf_op jit(solution)/shard_map/ppermute | solution.py:194
  154.4 17.8 %collective-permute-start.12 = (f32[64,256]{1,0:T(8,128)S(1)}, f32[64,256]{1,0:T(8,128)S(1)}, u32[]{:S(2)}, u32[]{:S(2)}) collective-permute-start(f32[64,256]{1,0:T(8,128)S(1)} %add_add_fusion), channel_id=1, source_target_pairs={{0,16},{8,24},{16,0},{24,8},{32,48},{40,56},{48,32},{56,40},{64,80... | collective-permute-start | bytes 196616 | tf_op jit(solution)/shard_map/ppermute | solution.py:194
  154.9 18.7 %collective-permute-start.11 = (f32[64,256]{1,0:T(8,128)S(1)}, f32[64,256]{1,0:T(8,128)S(1)}, u32[]{:S(2)}, u32[]{:S(2)}) collective-permute-start(f32[64,256]{1,0:T(8,128)S(1)} %add_add_fusion), channel_id=1, source_target_pairs={{0,48},{8,56},{16,32},{24,40},{32,16},{40,24},{48,0},{56,8},{64,11... | collective-permute-start | bytes 196616 | tf_op jit(solution)/shard_map/ppermute | solution.py:194

commit v5 on v4

--- a/solution.py
+++ b/solution.py
@@ -39,71 +39,60 @@
     return jnp.stack([turns_first, turns_second]), tile, picked, placed
 
 
-def spread_kernel(flipped, sources, turns_ref, tile_ref, pick_ref, place_ref, tiles_ref, *refs):
-    source_refs, out_refs = refs[:sources], refs[sources:-3]
+def spread_kernel(flipped, half, given, turns_ref, tile_ref, pick_ref, place_ref, tiles_ref, *refs):
+    source_ref, out_ref = refs[0], refs[1 + given]
     total_ref, held_ref, sems = refs[-3:]
     slots = tiles_ref.shape[0]
     wide = 2 * UNROLL
-    middle = turns_ref[0]
-    stop = middle + turns_ref[1]
-
-    @pl.loop(0, stop)
+    start = turns_ref[0] * half
+    stop = start + turns_ref[half]
+
+    @pl.loop(start, stop)
     def _(turn):
         for step in range(wide):
             slot = turn * wide + step
             tile = jnp.minimum(tile_ref[slot], slots - 1)
             pltpu.make_async_copy(tiles_ref.at[tile], held_ref.at[slot], sems.at[turn]).start()
 
-    total_ref[...] = jnp.zeros_like(total_ref)
+    total_ref[...] = refs[1][...] if given else jnp.zeros_like(total_ref)
 
     def tile_of(slot):
         return held_ref[slot] * (tile_ref[slot] < slots).astype(jnp.bfloat16)
 
-    def add_turns(start, end, source_ref):
-        def rows_of(slot):
-            return source_ref[pl.ds(pl.multiple_of(pick_ref[slot] * BLOCK, BLOCK), BLOCK), :]
-
-        @pl.loop(start, end)
-        def _(turn):
-            window = pl.ds(turn * wide, wide)
-            pltpu.make_async_copy(tiles_ref.at[pl.ds(0, wide)], held_ref.at[window], sems.at[turn]).wait()
-            for step in range(UNROLL):
-                first = turn * wide + 2 * step
-                rows = jnp.concatenate([rows_of(first), rows_of(first + 1)], axis=0)
-                tiles = [tile_of(first), tile_of(first + 1)]
-                if flipped:
-                    product = lax.dot_general(
-                        jnp.concatenate(tiles, axis=0),
-                        rows,
-                        (((0,), (0,)), ((), ())),
-                        preferred_element_type=jnp.float32,
-                    )
-                else:
-                    product = jnp.dot(jnp.concatenate(tiles, axis=1), rows, preferred_element_type=jnp.float32)
-                total_ref[place_ref[first]] += product
-
-    if sources == 1:
-        add_turns(0, stop, source_refs[0])
-    else:
-        add_turns(0, middle, source_refs[0])
-        add_turns(middle, stop, source_refs[1])
-    part = total_ref.shape[0] // len(out_refs)
-    for i, out_ref in enumerate(out_refs):
-        out_ref[...] = total_ref[i * part : (i + 1) * part].astype(out_ref.dtype)
-
-
-def spread(plan, tiles, sources, places, out_types, flipped):
-    width = sources[0].shape[1]
+    def rows_of(slot):
+        return source_ref[pl.ds(pl.multiple_of(pick_ref[slot] * BLOCK, BLOCK), BLOCK), :]
+
+    @pl.loop(start, stop)
+    def _(turn):
+        window = pl.ds(turn * wide, wide)
+        pltpu.make_async_copy(tiles_ref.at[pl.ds(0, wide)], held_ref.at[window], sems.at[turn]).wait()
+        for step in range(UNROLL):
+            first = turn * wide + 2 * step
+            rows = jnp.concatenate([rows_of(first), rows_of(first + 1)], axis=0)
+            tiles = [tile_of(first), tile_of(first + 1)]
+            if flipped:
+                product = lax.dot_general(
+                    jnp.concatenate(tiles, axis=0), rows, (((0,), (0,)), ((), ())), preferred_element_type=jnp.float32
+                )
+            else:
+                product = jnp.dot(jnp.concatenate(tiles, axis=1), rows, preferred_element_type=jnp.float32)
+            total_ref[place_ref[first]] += product
+
+    if total_ref is not out_ref:
+        out_ref[...] = total_ref[...].astype(out_ref.dtype)
+
+
+def spread(plan, half, tiles, source, places, given, out_type, flipped):
+    width = source.shape[1]
     halves = plan[1].shape[0]
     in_vmem = pl.BlockSpec(memory_space=pltpu.VMEM)
-    part = places // len(out_types)
     return pl.pallas_call(
-        functools.partial(spread_kernel, flipped, len(sources)),
-        out_shape=[jax.ShapeDtypeStruct((part, BLOCK, width), out_type) for out_type in out_types],
+        functools.partial(spread_kernel, flipped, half, len(given)),
+        out_shape=jax.ShapeDtypeStruct((places, BLOCK, width), out_type),
         in_specs=[pl.BlockSpec(memory_space=pltpu.SMEM)] * 4
         + [pl.BlockSpec(memory_space=pltpu.HBM)]
-        + [in_vmem] * len(sources),
-        out_specs=[in_vmem] * len(out_types),
+        + [in_vmem] * (1 + len(given)),
+        out_specs=in_vmem,
         scratch_shapes=[
             pltpu.VMEM((places, BLOCK, width), jnp.float32),
             pltpu.VMEM((halves, BLOCK, BLOCK), tiles.dtype),
@@ -111,10 +100,10 @@
         ],
         compiler_params=pltpu.CompilerParams(vmem_limit_bytes=SCOPE),
         cost_estimate=pl.CostEstimate(
-            flops=2 * tiles.size * width, bytes_accessed=2 * (tiles.size + len(sources) * sources[0].size), transcendentals=0
+            flops=tiles.size * width, bytes_accessed=tiles.size + 2 * source.size, transcendentals=0
         ),
-        name="spread_back" if flipped else "spread_forward",
-    )(*plan, tiles, *sources)
+        name=f"spread_{'back' if flipped else 'forward'}_{half}",
+    )(*plan, tiles, source, *given)
 
 
 def split(value):
@@ -226,13 +215,13 @@
     forward_plan = pair_plan(
         away * row_blocks + row_index, row_index, col_own, count, 2 * row_blocks
     )
-    col_place = away * col_blocks + col_own
-    back_plan = pair_plan(col_place, col_place, row_index, count, 2 * col_blocks)
+    back_plan = pair_plan((1 - away) * col_blocks + col_own, col_own, row_index, count, 2 * col_blocks)
 
     near = lax.all_to_all(copies_of(node_features, chips), "dom", 0, 0, axis_index_groups=same_core, tiled=True)
     far = exchange(near, "dom", 1)
     near, far = near.reshape(chips * rows, width), far.reshape(chips * rows, width)
-    (partial,) = spread(forward_plan, tiles, [near, far], row_blocks, [jnp.bfloat16], False)
+    partial = spread(forward_plan, 0, tiles, near, row_blocks, [], jnp.float32, False)
+    partial = spread(forward_plan, 1, tiles, far, row_blocks, [partial], jnp.bfloat16, False)
     parts = lax.all_to_all(partial.reshape(rep_size, rows, width), "rep", 0, 0, tiled=True)
     in_vmem = pl.BlockSpec(memory_space=pltpu.VMEM)
     output, grads, term = pl.pallas_call(
@@ -260,11 +249,9 @@
     term = (term + exchange(term, *across[1])) + (exchange(term, *across[2]) + both)
     grads, term = lax.optimization_barrier((grads, term))
 
-    mine, other = spread(
-        back_plan, tiles, [grads], 2 * col_blocks, [jnp.float32, jnp.bfloat16], True
-    )
-    mine, other = mine.reshape(chips, rows, width), other.reshape(chips, rows, width)
+    other = spread(back_plan, 0, tiles, grads, col_blocks, [], jnp.bfloat16, True).reshape(chips, rows, width)
     other = exchange(other, "dom", 1)
+    mine = spread(back_plan, 1, tiles, grads, col_blocks, [], jnp.float32, True).reshape(chips, rows, width)
     joined = pl.pallas_call(
         join_kernel,
         out_shape=pltpu.HBM((chips, rows, width), jnp.bfloat16),

time: 175 us -> 174 us (level); the launches traced: 176 us -> 172 us
  starting transfers between devices: 41.4 us -> 30.6 us
  Pallas kernels: 25.8 us -> 31.4 us
    ppermute x14, starting transfers between devices: 24.4 us -> 16.5 us  [exchange(): lax.ppermute(value, axis, [(place, place ^ bit) for place in range(size)])]
    pallas_call x2 -> x4, Pallas kernels: 18.1 us -> 23.7 us  [spread(): pl.pallas_call(functools.partial(spread_kernel, flipped, half, len(given)...]
    all_to_all x1, starting transfers between devices: 6.5 us -> 3.61 us  [body(): lax.all_to_all(joined, 'dom', 0, 0, axis_index_groups=same_core, tiled=True)]
  transfers between devices with their start and end apart: 17 -> 17, of which waited for: 13 -> 11; matrix products, arithmetic and copies ran while one was open for 3% -> 3% of each run, Pallas kernels for 0% -> 6%
where the time goes in v5:
time: 174 us; the launch traced here: 172 us
  waiting for transfers between devices  64.3 us (37%)
  blocking collectives  36.4 us (21%)
  Pallas kernels  31.4 us (18%)
  starting transfers between devices  30.6 us (18%)
  other arithmetic  4.73 us (3%)
  between operations  4.23 us (2%)
    ppermute x14, waiting for transfers between devices, exchange(): lax.ppermute(value, axis, [(place, place ^ bit) for place in range(size)])  42.4 us
    all_to_all x1, blocking collectives, body(): lax.all_to_all(partial.reshape(rep_size, rows, width), 'rep', 0, 0, tiled...  36.4 us
    pallas_call x4, Pallas kernels, spread(): pl.pallas_call(functools.partial(spread_kernel, flipped, half, len(given)...  23.7 us
    all_to_all x1, waiting for transfers between devices, body(): lax.all_to_all(copies_of(node_features, chips), 'dom', 0, 0, axis_index_g...  21.8 us
    ppermute x14, starting transfers between devices, exchange(): lax.ppermute(value, axis, [(place, place ^ bit) for place in range(size)])  16.5 us
    all_to_all x1, starting transfers between devices, body(): lax.all_to_all(copies_of(node_features, chips), 'dom', 0, 0, axis_index_g...  6.89 us
    all_to_all x1, starting transfers between devices, body(): lax.all_to_all(grads, 'rep', 0, 0, tiled=True)  3.61 us
    all_to_all x1, starting transfers between devices, body(): lax.all_to_all(joined, 'dom', 0, 0, axis_index_groups=same_core, tiled=True)  3.61 us
  transfers between devices with their start and end apart: 17, of which 11 were waited for; matrix products, arithmetic and copies ran while one was open for 3% of the time, Pallas kernels for 6%

profile of v5, /device:TPU:1, one launch (start us, length us, event | category | flops | bytes accessed | tf_op | source)
XLA Modules:
  0.0 171.7 jit_solution(5451642410444524396)
XLA Ops:
  0.6 2.4 %copies.1 = bf16[8,512,256]{2,1,0:T(8,128)(2,1)} custom-call(bf16[512,256]{1,0:T(8,128)(2,1)} %value_ref.1), custom_call_target="tpu_custom_call" | custom-call | tf_op jit(solution)/shard_map/copies/pallas_call | solution.py:123
  3.0 6.9 %all-to-all-start = ((bf16[8,512,256]{2,1,0:T(8,128)(2,1)}), bf16[8,512,256]{2,1,0:T(8,128)(2,1)S(1)}, u32[]{:S(2)}, u32[]{:S(2)}) async-start(bf16[8,512,256]{2,1,0:T(8,128)(2,1)} %copies.1), calls=%async_computation | async-start | bytes 4194304 | tf_op jit(solution)/shard_map/all_to_all | solution.py:220
  10.7 0.7 select_reduce_fusion.11
  12.2 0.7 select_reduce_fusion.13
  14.2 21.8 %all-to-all-done = bf16[8,512,256]{2,1,0:T(8,128)(2,1)S(1)} async-done(((bf16[8,512,256]{2,1,0:T(8,128)(2,1)}), bf16[8,512,256]{2,1,0:T(8,128)(2,1)S(1)}, u32[]{:S(2)}, u32[]{:S(2)}) %all-to-all-start) | async-done | bytes 2097184 | tf_op jit(solution)/shard_map/all_to_all | solution.py:220
  36.1 0.8 collective-permute-start
  37.9 1.2 select_reduce_fusion
  39.1 5.5 %spread_forward_0.1.refs_1_ = f32[32,128,256]{2,1,0:T(8,128)S(1)} custom-call(s32[2]{0:T(128)S(1)} %pad_add_fusion.turns_ref, s32[640]{0:T(1024)S(1)} %broadcast_add_fusion.1.tile_ref, s32[640]{0:T(1024)S(1)} %get-tuple-element.22.pick_ref, s32[640]{0:T(1024)S(1)} %get-tuple-element.23.place_ref, bf16[512,128,128]{2,1,0:T(8,128)(2,1)} %bitcast.24, ...), custom_call_target="tpu_custom_call" | custom-call | flops 2147483648 | bytes 10485760 | tf_op jit(solution)/shard_map/spread_forward_0/pallas_call | solution.py:89
  44.7 6.2 %spread_forward_1.1 = bf16[32,128,256]{2,1,0:T(8,128)(2,1)S(1)} custom-call(s32[2]{0:T(128)S(1)} %pad_add_fusion.turns_ref, s32[640]{0:T(1024)S(1)} %broadcast_add_fusion.1.tile_ref, s32[640]{0:T(1024)S(1)} %get-tuple-element.22.pick_ref, s32[640]{0:T(1024)S(1)} %get-tuple-element.23.place_ref, bf16[512,128,128]{2,1,0:T(8,128)(2,1)} %bitcast.25, ...), custom_call_target="tpu_custom_call" | custom-call | flops 2147483648 | bytes 10485760 | tf_op jit(solution)/shard_map/spread_forward_1/pallas_call | solution.py:89
  50.9 36.4 %all_to_all.20.parts_ref = bf16[8,512,256]{2,1,0:T(8,128)(2,1)S(1)} all-to-all(bf16[8,512,256]{2,1,0:T(8,128)(2,1)S(1)} %bitcast.21), channel_id=1, replica_groups=mesh['dom'=16,'rep'=8] {'rep'}, dimensions={0} | all-to-all | bytes 4194304 | tf_op jit(solution)/shard_map/all_to_all | solution.py:225
  87.4 2.8 %middle.1 = (bf16[512,256]{1,0:T(8,128)(2,1)}, bf16[8,512,256]{2,1,0:T(8,128)(2,1)}, f32[256,256]{1,0:T(8,128)S(1)}) custom-call(bf16[8,512,256]{2,1,0:T(8,128)(2,1)S(1)} %all_to_all.20.parts_ref, bf16[256,256]{1,0:T(8,128)(2,1)S(1)} %copy-done, bf16[512,256]{1,0:T(8,128)(2,1)S(1)} %copy-done.1), custom_call_target="tpu_custom_call" | custom-call | tf_op jit(solution)/shard_map/middle/pallas_call | solution.py:227
  90.1 3.6 %all-to-all-start.2 = ((bf16[8,512,256]{2,1,0:T(8,128)(2,1)}), bf16[8,512,256]{2,1,0:T(8,128)(2,1)S(1)}, u32[]{:S(2)}, u32[]{:S(2)}) async-start(bf16[8,512,256]{2,1,0:T(8,128)(2,1)} %get-tuple-element.13), calls=%async_computation.2 | async-start | bytes 4194304 | tf_op jit(solution)/shard_map/all_to_all | solution.py:240
  93.9 4.4 %collective-permute-done.1 = f32[128,256]{1,0:T(8,128)S(1)} collective-permute-done((f32[128,256]{1,0:T(8,128)S(1)}, f32[128,256]{1,0:T(8,128)S(1)}, u32[]{:S(2)}, u32[]{:S(2)}) %collective-permute-start.1) | collective-permute-done | bytes 131104 | tf_op jit(solution)/shard_map/ppermute | solution.py:183
  98.4 0.6 collective-permute-start.2
  99.0 4.3 %collective-permute-done.2 = f32[64,256]{1,0:T(8,128)S(1)} collective-permute-done((f32[64,256]{1,0:T(8,128)S(1)}, f32[64,256]{1,0:T(8,128)S(1)}, u32[]{:S(2)}, u32[]{:S(2)}) %collective-permute-start.2) | collective-permute-done | bytes 65568 | tf_op jit(solution)/shard_map/ppermute | solution.py:183
  103.4 2.4 %collective-permute-start.3 = (f32[64,256]{1,0:T(8,128)S(1)}, f32[64,256]{1,0:T(8,128)S(1)}, u32[]{:S(2)}, u32[]{:S(2)}) collective-permute-start(f32[64,256]{1,0:T(8,128)S(1)} %select_add_fusion.1), channel_id=1, source_target_pairs={{0,8},{8,0},{16,24},{24,16},{32,40},{40,32},{48,56},{56,48},{64,72... | collective-permute-start | bytes 196616 | tf_op jit(solution)/shard_map/ppermute | solution.py:183
  106.7 1.4 collective-permute-start.6
  108.0 1.7 collective-permute-start.5
  110.1 13.9 %collective-permute-done.6 = f32[64,256]{1,0:T(8,128)S(1)} collective-permute-done((f32[64,256]{1,0:T(8,128)S(1)}, f32[64,256]{1,0:T(8,128)S(1)}, u32[]{:S(2)}, u32[]{:S(2)}) %collective-permute-start.6) | collective-permute-done | bytes 65568 | tf_op jit(solution)/shard_map/ppermute | solution.py:183
  124.0 6.3 %spread_back_0.1 = bf16[32,128,256]{2,1,0:T(8,128)(2,1)S(1)} custom-call(s32[2]{0:T(128)S(1)} %pad_add_fusion.1.turns_ref, s32[640]{0:T(1024)S(1)} %broadcast_add_fusion.tile_ref, s32[640]{0:T(1024)S(1)} %get-tuple-element.24.pick_ref, s32[640]{0:T(1024)S(1)} %get-tuple-element.21.place_ref, bf16[512,128,128]{2,1,0:T(8,128)(2,1)} %bitcast.26, ...), custom_call_target="tpu_custom_call" | custom-call | flops 2147483648 | bytes 10485760 | tf_op jit(solution)/shard_map/spread_back_0/pallas_call | solution.py:89
  131.0 5.6 %spread_back_1.1 = f32[32,128,256]{2,1,0:T(8,128)S(1)} custom-call(s32[2]{0:T(128)S(1)} %pad_add_fusion.1.turns_ref, s32[640]{0:T(1024)S(1)} %broadcast_add_fusion.tile_ref, s32[640]{0:T(1024)S(1)} %get-tuple-element.24.pick_ref, s32[640]{0:T(1024)S(1)} %get-tuple-element.21.place_ref, bf16[512,128,128]{2,1,0:T(8,128)(2,1)} %bitcast.27, ...), custom_call_target="tpu_custom_call" | custom-call | flops 2147483648 | bytes 10485760 | tf_op jit(solution)/shard_map/spread_back_1/pallas_call | solution.py:89
  136.6 1.5 join.1
  138.1 3.6 %all-to-all-start.3 = ((bf16[8,512,256]{2,1,0:T(8,128)(2,1)}), bf16[8,512,256]{2,1,0:T(8,128)(2,1)S(1)}, u32[]{:S(2)}, u32[]{:S(2)}) async-start(bf16[8,512,256]{2,1,0:T(8,128)(2,1)} %join.1), calls=%async_computation.3 | async-start | bytes 4194304 | tf_op jit(solution)/shard_map/all_to_all | solution.py:265
  141.7 3.7 %collective-permute-start.10 = (f32[64,256]{1,0:T(8,128)S(1)}, f32[64,256]{1,0:T(8,128)S(1)}, u32[]{:S(2)}, u32[]{:S(2)}) collective-permute-start(f32[64,256]{1,0:T(8,128)S(1)} %add_add_fusion.1), channel_id=1, source_target_pairs={{0,3},{1,2},{2,1},{3,0},{4,7},{5,6},{6,5},{7,4},{8,11},{9,10},{10,... | collective-permute-start | bytes 196616 | tf_op jit(solution)/shard_map/ppermute | solution.py:183
  145.4 1.3 collective-permute-start.8
  147.2 1.6 collective-permute-done.9
  148.8 1.6 collective-permute-done.8
  150.4 2.8 %collective-permute-start.13 = (f32[64,256]{1,0:T(8,128)S(1)}, f32[64,256]{1,0:T(8,128)S(1)}, u32[]{:S(2)}, u32[]{:S(2)}) collective-permute-start(f32[64,256]{1,0:T(8,128)S(1)} %add_add_fusion), channel_id=1, source_target_pairs={{0,32},{8,40},{16,48},{24,56},{32,0},{40,8},{48,16},{56,24},{64,96... | collective-permute-start | bytes 196616 | tf_op jit(solution)/shard_map/ppermute | solution.py:183
  154.1 14.2 %collective-permute-done.13 = f32[64,256]{1,0:T(8,128)S(1)} collective-permute-done((f32[64,256]{1,0:T(8,128)S(1)}, f32[64,256]{1,0:T(8,128)S(1)}, u32[]{:S(2)}, u32[]{:S(2)}) %collective-permute-start.13) | collective-permute-done | bytes 65568 | tf_op jit(solution)/shard_map/ppermute | solution.py:183
  168.8 1.1 collective-permute-done.11
  169.9 0.7 pad_maximum_fusion
  170.6 1.1 last.1
  (51 shorter events, 4.7 us)
Async XLA Ops:
  3.0 7.6 %copy-start.3 = (s32[1,1,512]{2,1,0:T(1,128)S(1)}, s32[1,1,512]{2,1,0:T(1,128)}, u32[]{:S(2)}) copy-start(s32[1,1,512]{2,1,0:T(1,128)} %param.11) | copy-start | bytes 6148
  3.0 9.0 %copy-start.2 = (s32[1,1,512]{2,1,0:T(1,128)S(1)}, s32[1,1,512]{2,1,0:T(1,128)}, u32[]{:S(2)}) copy-start(s32[1,1,512]{2,1,0:T(1,128)} %param.10) | copy-start | bytes 6148
  3.0 33.0 %all-to-all-start = ((bf16[8,512,256]{2,1,0:T(8,128)(2,1)}), bf16[8,512,256]{2,1,0:T(8,128)(2,1)S(1)}, u32[]{:S(2)}, u32[]{:S(2)}) async-start(bf16[8,512,256]{2,1,0:T(8,128)(2,1)} %copies.1), calls=%async_computation | async-start | bytes 4194304 | tf_op jit(solution)/shard_map/all_to_all | solution.py:220
  36.1 8.6 %collective-permute-start = (bf16[8,512,256]{2,1,0:T(8,128)(2,1)S(1)}, bf16[8,512,256]{2,1,0:T(8,128)(2,1)S(1)}, u32[]{:S(2)}, u32[]{:S(2)}) collective-permute-start(bf16[8,512,256]{2,1,0:T(8,128)(2,1)S(1)} %all-to-all-done), channel_id=1, source_target_pairs={{0,8},{8,0},{16,24},{24,16},{32,40},{40,32},{48,56},{56,48},{64,72... | collective-permute-start | bytes 6291464 | tf_op jit(solution)/shard_map/ppermute | solution.py:183
  50.9 36.4 %copy-start = (bf16[256,256]{1,0:T(8,128)(2,1)S(1)}, bf16[256,256]{1,0:T(8,128)(2,1)}, u32[]{:S(2)}) copy-start(bf16[256,256]{1,0:T(8,128)(2,1)} %weight_ref.3) | copy-start | bytes 393220
  50.9 36.4 %copy-start.1 = (bf16[512,256]{1,0:T(8,128)(2,1)S(1)}, bf16[512,256]{1,0:T(8,128)(2,1)}, u32[]{:S(2)}) copy-start(bf16[512,256]{1,0:T(8,128)(2,1)} %cotangent_ref.1) | copy-start | bytes 786436
  90.1 33.9 %all-to-all-start.2 = ((bf16[8,512,256]{2,1,0:T(8,128)(2,1)}), bf16[8,512,256]{2,1,0:T(8,128)(2,1)S(1)}, u32[]{:S(2)}, u32[]{:S(2)}) async-start(bf16[8,512,256]{2,1,0:T(8,128)(2,1)} %get-tuple-element.13), calls=%async_computation.2 | async-start | bytes 4194304 | tf_op jit(solution)/shard_map/all_to_all | solution.py:240
  93.8 4.5 %collective-permute-start.1 = (f32[128,256]{1,0:T(8,128)S(1)}, f32[128,256]{1,0:T(8,128)S(1)}, u32[]{:S(2)}, u32[]{:S(2)}) collective-permute-start(f32[128,256]{1,0:T(8,128)S(1)} %slice_select_fusion), channel_id=1, source_target_pairs={{0,16},{8,24},{16,0},{24,8},{32,48},{40,56},{48,32},{56,40},{64,80... | collective-permute-start | bytes 393224 | tf_op jit(solution)/shard_map/ppermute | solution.py:183
  98.4 5.0 %collective-permute-start.2 = (f32[64,256]{1,0:T(8,128)S(1)}, f32[64,256]{1,0:T(8,128)S(1)}, u32[]{:S(2)}, u32[]{:S(2)}) collective-permute-start(f32[64,256]{1,0:T(8,128)S(1)} %slice_select_fusion.1), channel_id=1, source_target_pairs={{0,32},{8,40},{16,48},{24,56},{32,0},{40,8},{48,16},{56,24},{64,96... | collective-permute-start | bytes 196616 | tf_op jit(solution)/shard_map/ppermute | solution.py:183
  103.4 3.3 %collective-permute-start.3 = (f32[64,256]{1,0:T(8,128)S(1)}, f32[64,256]{1,0:T(8,128)S(1)}, u32[]{:S(2)}, u32[]{:S(2)}) collective-permute-start(f32[64,256]{1,0:T(8,128)S(1)} %select_add_fusion.1), channel_id=1, source_target_pairs={{0,8},{8,0},{16,24},{24,16},{32,40},{40,32},{48,56},{56,48},{64,72... | collective-permute-start | bytes 196616 | tf_op jit(solution)/shard_map/ppermute | solution.py:183
  106.7 17.3 %collective-permute-start.6 = (f32[64,256]{1,0:T(8,128)S(1)}, f32[64,256]{1,0:T(8,128)S(1)}, u32[]{:S(2)}, u32[]{:S(2)}) collective-permute-start(f32[64,256]{1,0:T(8,128)S(1)} %add.254), channel_id=1, source_target_pairs={{0,68},{1,69},{2,70},{3,71},{4,64},{5,65},{6,66},{7,67},{8,76},{9,... | collective-permute-start | bytes 196616 | tf_op jit(solution)/shard_map/ppermute | solution.py:183
  108.0 15.9 %collective-permute-start.5 = (f32[64,256]{1,0:T(8,128)S(1)}, f32[64,256]{1,0:T(8,128)S(1)}, u32[]{:S(2)}, u32[]{:S(2)}) collective-permute-start(f32[64,256]{1,0:T(8,128)S(1)} %add.254), channel_id=1, source_target_pairs={{0,4},{1,5},{2,6},{3,7},{4,0},{5,1},{6,2},{7,3},{8,12},{9,13},{10,... | collective-permute-start | bytes 196616 | tf_op jit(solution)/shard_map/ppermute | solution.py:183
  109.7 14.2 %collective-permute-start.4 = (f32[64,256]{1,0:T(8,128)S(1)}, f32[64,256]{1,0:T(8,128)S(1)}, u32[]{:S(2)}, u32[]{:S(2)}) collective-permute-start(f32[64,256]{1,0:T(8,128)S(1)} %add.254), channel_id=1, source_target_pairs={{0,64},{8,72},{16,80},{24,88},{32,96},{40,104},{48,112},{56,120},{... | collective-permute-start | bytes 196616 | tf_op jit(solution)/shard_map/ppermute | solution.py:183
  130.4 6.2 %collective-permute-start.7 = (bf16[8,512,256]{2,1,0:T(8,128)(2,1)S(1)}, bf16[8,512,256]{2,1,0:T(8,128)(2,1)S(1)}, u32[]{:S(2)}, u32[]{:S(2)}) collective-permute-start(bf16[8,512,256]{2,1,0:T(8,128)(2,1)S(1)} %bitcast.22), channel_id=1, source_target_pairs={{0,8},{8,0},{16,24},{24,16},{32,40},{40,32},{48,56},{56,48},{64,72... | collective-permute-start | bytes 6291464 | tf_op jit(solution)/shard_map/ppermute | solution.py:183
  138.1 32.6 %all-to-all-start.3 = ((bf16[8,512,256]{2,1,0:T(8,128)(2,1)}), bf16[8,512,256]{2,1,0:T(8,128)(2,1)S(1)}, u32[]{:S(2)}, u32[]{:S(2)}) async-start(bf16[8,512,256]{2,1,0:T(8,128)(2,1)} %join.1), calls=%async_computation.3 | async-start | bytes 4194304 | tf_op jit(solution)/shard_map/all_to_all | solution.py:265
  141.7 5.5 %collective-permute-start.10 = (f32[64,256]{1,0:T(8,128)S(1)}, f32[64,256]{1,0:T(8,128)S(1)}, u32[]{:S(2)}, u32[]{:S(2)}) collective-permute-start(f32[64,256]{1,0:T(8,128)S(1)} %add_add_fusion.1), channel_id=1, source_target_pairs={{0,3},{1,2},{2,1},{3,0},{4,7},{5,6},{6,5},{7,4},{8,11},{9,10},{10,... | collective-permute-start | bytes 196616 | tf_op jit(solution)/shard_map/ppermute | solution.py:183
  145.4 3.4 %collective-permute-start.9 = (f32[64,256]{1,0:T(8,128)S(1)}, f32[64,256]{1,0:T(8,128)S(1)}, u32[]{:S(2)}, u32[]{:S(2)}) collective-permute-start(f32[64,256]{1,0:T(8,128)S(1)} %add_add_fusion.1), channel_id=1, source_target_pairs={{0,1},{1,0},{2,3},{3,2},{4,5},{5,4},{6,7},{7,6},{8,9},{9,8},{10,11... | collective-permute-start | bytes 196616 | tf_op jit(solution)/shard_map/ppermute | solution.py:183
  145.4 5.0 %collective-permute-start.8 = (f32[64,256]{1,0:T(8,128)S(1)}, f32[64,256]{1,0:T(8,128)S(1)}, u32[]{:S(2)}, u32[]{:S(2)}) collective-permute-start(f32[64,256]{1,0:T(8,128)S(1)} %add_add_fusion.1), channel_id=1, source_target_pairs={{0,2},{1,3},{2,0},{3,1},{4,6},{5,7},{6,4},{7,5},{8,10},{9,11},{10,... | collective-permute-start | bytes 196616 | tf_op jit(solution)/shard_map/ppermute | solution.py:183
  150.4 17.8 %collective-permute-start.13 = (f32[64,256]{1,0:T(8,128)S(1)}, f32[64,256]{1,0:T(8,128)S(1)}, u32[]{:S(2)}, u32[]{:S(2)}) collective-permute-start(f32[64,256]{1,0:T(8,128)S(1)} %add_add_fusion), channel_id=1, source_target_pairs={{0,32},{8,40},{16,48},{24,56},{32,0},{40,8},{48,16},{56,24},{64,96... | collective-permute-start | bytes 196616 | tf_op jit(solution)/shard_map/ppermute | solution.py:183
  153.2 15.6 %collective-permute-start.12 = (f32[64,256]{1,0:T(8,128)S(1)}, f32[64,256]{1,0:T(8,128)S(1)}, u32[]{:S(2)}, u32[]{:S(2)}) collective-permute-start(f32[64,256]{1,0:T(8,128)S(1)} %add_add_fusion), channel_id=1, source_target_pairs={{0,16},{8,24},{16,0},{24,8},{32,48},{40,56},{48,32},{56,40},{64,80... | collective-permute-start | bytes 196616 | tf_op jit(solution)/shard_map/ppermute | solution.py:183
  153.8 16.1 %collective-permute-start.11 = (f32[64,256]{1,0:T(8,128)S(1)}, f32[64,256]{1,0:T(8,128)S(1)}, u32[]{:S(2)}, u32[]{:S(2)}) collective-permute-start(f32[64,256]{1,0:T(8,128)S(1)} %add_add_fusion), channel_id=1, source_target_pairs={{0,48},{8,56},{16,32},{24,40},{32,16},{40,24},{48,0},{56,8},{64,11... | collective-permute-start | bytes 196616 | tf_op jit(solution)/shard_map/ppermute | solution.py:183
